TPU v7x, 32 devices: a whole 2x2x4 slice. The times are simulated.
32 devices in a mesh: ep: 8 (over z, y), zr: 4 (over x, core).
Axes of the slice: x: 2, y: 2, z: 4, core: 2. Of those that a mesh axis runs over, the one named last changes fastest.
Arguments:
- tokens: bfloat16 [4096, 1024], P(('ep', 'zr')), may hold values from -6 to 6
- cotangent: bfloat16 [4096, 1024], P(('ep', 'zr')), may hold values from -6 to 6
- gates: bfloat16 [4096, 2], P(('ep', 'zr')), may hold values from 0.099609375 to 0.8984375
- experts: int32 [4096, 2], P(('ep', 'zr')), may hold values from 0 to 7, all different within a row; in each aligned block of 128 rows (0 to 127, 128 to 255, ...) at most 48 rows name the same one
- keep: int32 [4096, 2], P(('ep', 'zr')), may hold values 0 or 1
- gate_w: bfloat16 [8, 1024, 1024], P('ep', None, 'zr'), may hold values from -0.1875 to 0.1875
- up_w: bfloat16 [8, 1024, 1024], P('ep', None, 'zr'), may hold values from -0.1875 to 0.1875
- down_w: bfloat16 [8, 1024, 1024], P('ep', 'zr'), may hold values from -0.1875 to 0.1875
Outputs:
- d_tokens: bfloat16 [4096, 1024], P(('ep', 'zr'))
- d_gates: bfloat16 [4096, 2], P(('ep', 'zr'))
- d_gate_w: bfloat16 [8, 1024, 1024], P('ep', None, 'zr')
- d_up_w: bfloat16 [8, 1024, 1024], P('ep', None, 'zr')
- d_down_w: bfloat16 [8, 1024, 1024], P('ep', 'zr')
Inputs may be any that keep to these rules, and one draw needn't show every extreme that they name: Each row names two different experts. Among the 128 rows of one device no expert is named more than 48 times, and in every draw some expert is named exactly 48 times by the rows of some device.
All inputs are finite; a program needn't handle non-finite values. No bound on the sum of `keep` on one device may be relied on, other than what follows from the above.
Results may differ from a plain program's by a relative error of at most 0.012.
Values may be sent and summed in bfloat16 or wider, within the bound.
No kernel may reach another device: no remote copies, remote signals or barrier semaphores. Data moves between devices by JAX's collectives and lax.ppermute only.
A program may use at most 64 MiB of HBM per device.

v0:
```python
import functools

import jax
import jax.numpy as jnp
from jax import lax
from jax.experimental import pallas as pl
from jax.experimental.pallas import tpu as pltpu
from jax.sharding import PartitionSpec as P


F32 = jnp.float32
BF16 = jnp.bfloat16
LANES = 128
VMEM_LIMIT = 24 * 1024 * 1024


def contract(a, b, dim_a, dim_b):
    return lax.dot_general(a, b, (((dim_a,), (dim_b,)), ((), ())), preferred_element_type=F32)


def send_kernel(n_experts, capacity, me_ref, exp_ref, keep_ref, gate_ref, tok_ref, cot_ref, *outs):
    rows = tok_ref.shape[0]
    table_ref, messages = outs[0], outs[1:]
    earlier = lax.broadcasted_iota(jnp.int32, (rows, rows), 0) < lax.broadcasted_iota(jnp.int32, (rows, rows), 1)
    weight = gate_ref[...].astype(F32) * keep_ref[...].astype(F32)
    ids = lax.broadcasted_iota(jnp.int32, (n_experts, rows), 0) ^ me_ref[0]
    named0 = exp_ref[0:1, :] == ids
    named1 = exp_ref[1:2, :] == ids
    named = named0 | named1
    w_of = jnp.where(named0, weight[0:1, :], 0.0) + jnp.where(named1, weight[1:2, :], 0.0)
    position = contract(jnp.where(named, 1.0, 0.0).astype(BF16), jnp.where(earlier, 1.0, 0.0).astype(BF16), 1, 0)
    position = jnp.where(named, position, -1.0)
    slots = lax.broadcasted_iota(jnp.int32, (capacity, rows), 0).astype(F32)
    for k in range(n_experts):
        hit = slots == position[k : k + 1, :]
        table = jnp.where(hit, 1.0, 0.0).astype(BF16)
        table_w = jnp.where(hit, w_of[k : k + 1, :], 0.0).astype(BF16)
        table_ref[k * capacity : (k + 1) * capacity, :] = table
        messages[k][0:capacity, :] = contract(table, tok_ref[...], 1, 0).astype(BF16)
        messages[k][capacity:, :] = contract(table_w, cot_ref[...], 1, 0).astype(BF16)


def grad_kernel(n_msgs, n_own, capacity, *refs):
    msgs = refs[:n_msgs]
    wg_refs, wu_refs, wd_refs = refs[n_msgs : n_msgs + 2], refs[n_msgs + 2 : n_msgs + 4], refs[n_msgs + 4 : n_msgs + 6]
    outs = refs[n_msgs + 6 :]
    back, (da_ref, db_ref, h_ref) = outs[:-3], outs[-3:]
    width = msgs[0].shape[1]
    x = jnp.concatenate([m[0:capacity, :] for m in msgs], axis=0)
    gw = jnp.concatenate([m[capacity:, :] for m in msgs], axis=0)
    part_x = None
    part_g = None
    for q in range(2):
        a = contract(x, wg_refs[q][...], 1, 0)
        b = contract(x, wu_refs[q][...], 1, 0)
        dh = contract(gw, wd_refs[q][...], 1, 1)
        sig = 1.0 / (1.0 + jnp.exp(-a))
        act = a * sig
        h = act * b
        da = (dh * b * sig * (1.0 + a * (1.0 - sig))).astype(BF16)
        db = (dh * act).astype(BF16)
        hidden = a.shape[1]
        cols = slice(q * hidden, (q + 1) * hidden)
        da_ref[:, cols] = da
        db_ref[:, cols] = db
        h_ref[:, cols] = h.astype(BF16)
        px = contract(da, wg_refs[q][...], 1, 1) + contract(db, wu_refs[q][...], 1, 1)
        pg = jnp.sum(h * dh, axis=1, keepdims=True)
        part_x = px if part_x is None else part_x + px
        part_g = pg if part_g is None else part_g + pg
    n_rows = n_own * capacity
    for p in range(n_msgs // n_own):
        rows = slice(p * n_rows, (p + 1) * n_rows)
        back[p][:, 0:width] = part_x[rows, :].astype(BF16)
        back[p][:, width:] = jnp.broadcast_to(part_g[rows, :], (n_rows, LANES)).astype(BF16)


def weight_kernel(counts, capacity, quarter, has_received, *refs):
    n_msgs = sum(counts)
    msgs, refs = refs[:n_msgs], refs[n_msgs:]
    das, refs = refs[: len(counts)], refs[len(counts) :]
    dbs, refs = refs[: len(counts)], refs[len(counts) :]
    hs, refs = refs[: len(counts)], refs[len(counts) :]
    received, outs = (refs[:3], refs[3:]) if has_received else (None, refs)
    hidden = outs[2].shape[0]
    cols = slice(quarter * hidden, (quarter + 1) * hidden)
    x = jnp.concatenate([m[0:capacity, :] for m in msgs], axis=0)
    gw = jnp.concatenate([m[capacity:, :] for m in msgs], axis=0)
    da = jnp.concatenate([r[:, cols] for r in das], axis=0)
    db = jnp.concatenate([r[:, cols] for r in dbs], axis=0)
    h = jnp.concatenate([r[:, cols] for r in hs], axis=0)
    results = (contract(x, da, 0, 0), contract(x, db, 0, 0), contract(h, gw, 0, 0))
    for i in range(3):
        total = results[i]
        if has_received:
            total = total + received[i][...].astype(F32)
        outs[i][...] = total.astype(BF16)


def sum_kernel(n_parts, capacity, *refs):
    total = refs[0][...].astype(F32)
    for p in range(1, n_parts):
        total = total + refs[p][...].astype(F32)
    for m, out in enumerate(refs[n_parts:]):
        out[...] = total[m * capacity : (m + 1) * capacity, :].astype(BF16)


def combine_kernel(n_experts, capacity, me_ref, exp_ref, keep_ref, gate_ref, table_ref, *refs):
    msgs, (dtok_ref, dgate_ref) = refs[:n_experts], refs[n_experts:]
    width = dtok_ref.shape[1]
    rows = jnp.concatenate([m[:, 0:width] for m in msgs], axis=0)
    dtok_ref[...] = contract(table_ref[...], rows, 0, 0).astype(BF16)
    d_gates = jnp.zeros(exp_ref.shape, F32)
    for k in range(n_experts):
        value = contract(msgs[k][:, width:], table_ref[k * capacity : (k + 1) * capacity, :], 0, 0)
        d_gates = d_gates + jnp.where(exp_ref[...] == (me_ref[0] ^ k), value[0 : exp_ref.shape[0], :], 0.0)
    d_gates = d_gates * keep_ref[...].astype(F32) / gate_ref[...].astype(F32)
    dgate_ref[...] = d_gates.astype(BF16)


def call(body, outs, n_in, smem=0, cost=None):
    vmem = pl.BlockSpec(memory_space=pltpu.VMEM)
    scalar = pl.BlockSpec(memory_space=pltpu.SMEM)
    return pl.pallas_call(
        body,
        out_shape=[jax.ShapeDtypeStruct(shape, BF16) for shape in outs],
        in_specs=[scalar] * smem + [vmem] * (n_in - smem),
        out_specs=[vmem] * len(outs),
        cost_estimate=cost,
        compiler_params=pltpu.CompilerParams(vmem_limit_bytes=VMEM_LIMIT),
    )


def groups_of(n_experts):
    half = n_experts // 2
    groups = ([0, 1, half], [k for k in range(2, half)] + [half + 1], list(range(half + 2, n_experts)))
    return {f"g{i}": g for i, g in enumerate(groups) if g}


def local_tiled(tokens, cotangent, gates, experts, keep, gate_w, up_w, down_w):
    return local_steps(tokens, cotangent, gates, experts, keep, gate_w, up_w, down_w)


def local_steps(tokens, cotangent, gates, experts, keep, gate_w, up_w, down_w):
    n_experts = lax.axis_size("ep")
    n_groups = lax.axis_size("zr")
    tok_rows, width = tokens.shape
    hidden = gate_w.shape[2]
    capacity = 3 * tok_rows // n_experts
    me = lax.axis_index("ep").astype(jnp.int32).reshape(1)
    route = (me, experts.T, keep.T, gates.T)

    def exchange(value, axis, size, bit):
        return lax.ppermute(value, axis, [(i, i ^ bit) for i in range(size)])

    def run(body, outs, *args, smem=0):
        return call(body, outs, len(args), smem=smem)(*args)

    weights = []
    for w in (gate_w, up_w, down_w):
        weights += [w[0], exchange(w[0], "zr", n_groups, 1)]

    outs = [(n_experts * capacity, tok_rows)] + [(2 * capacity, width)] * n_experts
    table, *sends = run(functools.partial(send_kernel, n_experts, capacity), outs, *route, tokens, cotangent, smem=1)
    mine = [exchange(sends[k], "ep", n_experts, k) if k else sends[0] for k in range(n_experts)]
    peers = list(range(2, n_groups, 2))
    theirs = [[exchange(mine[k], "zr", n_groups, r) for r in peers] for k in range(n_experts)]

    all_msgs, counts, das, dbs, hs, returned = [], [], [], [], [], {}
    for group in groups_of(n_experts).values():
        msgs = [mine[k] for k in group] + [theirs[k][p] for p in range(len(peers)) for k in group]
        n_rows, n_own = len(msgs) * capacity, len(group) * capacity
        outs = [(n_own, width + LANES)] * (1 + len(peers)) + [(n_rows, 2 * hidden)] * 3
        body = functools.partial(grad_kernel, len(msgs), len(group), capacity)
        *back, da, db, h = run(body, outs, *msgs, *weights)
        all_msgs, counts = all_msgs + msgs, counts + [len(msgs)]
        das, dbs, hs = das + [da], dbs + [db], hs + [h]
        parts = [back[0]] + [exchange(back[1 + p], "zr", n_groups, r) for p, r in enumerate(peers)]
        body = functools.partial(sum_kernel, len(parts), capacity)
        summed = run(body, [(capacity, width + LANES)] * len(group), *parts)
        for i, k in enumerate(group):
            returned[k] = exchange(summed[i], "ep", n_experts, k) if k else summed[i]

    w_outs = [(width, hidden), (width, hidden), (hidden, width)]
    w_args = all_msgs + das + dbs + hs
    partner = run(functools.partial(weight_kernel, counts, capacity, 1, False), w_outs, *w_args)
    w_args = w_args + [exchange(w, "zr", n_groups, 1) for w in partner]
    dwg, dwu, dwd = run(functools.partial(weight_kernel, counts, capacity, 0, True), w_outs, *w_args)

    outs = [(tok_rows, width), experts.T.shape]
    d_tokens, d_gates = run(
        functools.partial(combine_kernel, n_experts, capacity),
        outs,
        *route,
        table,
        *[returned[k] for k in range(n_experts)],
        smem=1,
    )
    return d_tokens, d_gates.T, dwg[None], dwu[None], dwd[None]


def route_tables(experts, keep, gates, n_experts, capacity):
    tok_rows = experts.shape[0]
    flat_exp = experts.reshape(-1)
    onehot = (flat_exp[:, None] == jnp.arange(n_experts, dtype=jnp.int32)[None, :]).astype(
        jnp.int32
    )
    before = jnp.cumsum(onehot, axis=0) - onehot
    position = jnp.sum(before * onehot, axis=1)
    dest = (flat_exp * capacity + position).reshape(tok_rows, 2)
    slot_ids = jnp.arange(n_experts * capacity, dtype=jnp.int32)
    matches = dest[None, :, :] == slot_ids[:, None, None]
    table = jnp.any(matches, axis=2).astype(jnp.bfloat16)
    weight = gates.astype(jnp.float32) * keep.astype(jnp.float32)
    slot_weight = jnp.sum(jnp.where(matches, weight[None, :, :], 0.0), axis=(1, 2))
    return (table, dest, slot_weight)


def expert_grads(slot_input_rows, slot_g, slot_w, wg, wu, wd):
    pre_a = jnp.dot(slot_input_rows, wg, preferred_element_type=jnp.float32)
    pre_b = jnp.dot(slot_input_rows, wu, preferred_element_type=jnp.float32)
    sig = 1.0 / (1.0 + jnp.exp(-pre_a))
    act = pre_a * sig
    hidden_activation = act * pre_b
    value_gradient = jnp.einsum("sd,hd->sh", slot_g, wd, preferred_element_type=jnp.float32)
    scale = slot_w.astype(jnp.float32)[:, None]
    dh = scale * value_gradient
    gate_branch_gradient = (dh * pre_b * sig * (1.0 + pre_a * (1.0 - sig))).astype(jnp.bfloat16)
    up_branch_gradient = (dh * act).astype(jnp.bfloat16)
    hidden_w = (scale * hidden_activation).astype(jnp.bfloat16)
    dwg = jnp.einsum(
        "sd,sh->dh", slot_input_rows, gate_branch_gradient, preferred_element_type=jnp.float32
    ).astype(jnp.bfloat16)
    dwu = jnp.einsum(
        "sd,sh->dh", slot_input_rows, up_branch_gradient, preferred_element_type=jnp.float32
    ).astype(jnp.bfloat16)
    dwd = jnp.einsum("sh,sd->hd", hidden_w, slot_g, preferred_element_type=jnp.float32).astype(
        jnp.bfloat16
    )
    part_x = jnp.einsum("sh,dh->sd", gate_branch_gradient, wg, preferred_element_type=jnp.float32)
    part_x = part_x + jnp.einsum(
        "sh,dh->sd", up_branch_gradient, wu, preferred_element_type=jnp.float32
    )
    partial_gate_rows = jnp.sum(hidden_activation * value_gradient, axis=1)
    return (dwg, dwu, dwd, part_x.astype(jnp.bfloat16), partial_gate_rows.astype(jnp.bfloat16))


def local_general(tokens, cotangent, gates, experts, keep, gate_w, up_w, down_w):
    n_experts = lax.axis_size("ep")
    n_groups = lax.axis_size("zr")
    tok_rows = tokens.shape[0]
    width = tokens.shape[1]
    capacity = max(2, 3 * tok_rows // n_experts)
    flat_width = capacity * width
    table, dest, slot_weight = route_tables(experts, keep, gates, n_experts, capacity)
    send_x = jnp.dot(table, tokens, preferred_element_type=jnp.float32).astype(jnp.bfloat16)
    send_g = jnp.dot(table, cotangent, preferred_element_type=jnp.float32).astype(jnp.bfloat16)
    send_x = send_x.reshape(1, n_experts, flat_width)
    send_g = send_g.reshape(1, n_experts, flat_width)
    send_w = slot_weight.astype(jnp.bfloat16).reshape(1, n_experts, capacity)
    moved = (
        lax.all_to_all(send_x, "ep", split_axis=1, concat_axis=1, tiled=True),
        lax.all_to_all(send_g, "ep", split_axis=1, concat_axis=1, tiled=True),
        lax.all_to_all(send_w, "ep", split_axis=1, concat_axis=1, tiled=True),
    )
    arrived = (
        lax.all_gather(moved[0], "zr", axis=0, tiled=True),
        lax.all_gather(moved[1], "zr", axis=0, tiled=True),
        lax.all_gather(moved[2], "zr", axis=0, tiled=True),
    )
    slot_input_rows = arrived[0].reshape(-1, width)
    slot_g = arrived[1].reshape(-1, width)
    slot_w = arrived[2].reshape(-1)
    dwg, dwu, dwd, part_x, partial_gate_rows = expert_grads(
        slot_input_rows, slot_g, slot_w, gate_w[0], up_w[0], down_w[0]
    )
    part_x = part_x.reshape(n_groups, n_experts, flat_width)
    partial_gate_rows = partial_gate_rows.reshape(n_groups, n_experts, capacity)
    summed = (
        lax.psum_scatter(
            part_x.astype(jnp.float32).astype(jnp.bfloat16), "zr", scatter_dimension=0, tiled=True
        ).astype(jnp.float32),
        lax.psum_scatter(
            partial_gate_rows.astype(jnp.float32).astype(jnp.bfloat16),
            "zr",
            scatter_dimension=0,
            tiled=True,
        ).astype(jnp.float32),
    )
    rounded = (summed[0].astype(jnp.bfloat16), summed[1].astype(jnp.bfloat16))
    returned = (
        lax.all_to_all(rounded[0], "ep", split_axis=1, concat_axis=1, tiled=True),
        lax.all_to_all(rounded[1], "ep", split_axis=1, concat_axis=1, tiled=True),
    )
    slot_dx = returned[0]
    slot_dg = returned[1]
    slot_dx = slot_dx.reshape(n_experts * capacity, width)
    slot_dg = slot_dg.reshape(n_experts * capacity)
    d_tokens = jnp.einsum("st,sd->td", table, slot_dx, preferred_element_type=jnp.float32).astype(
        jnp.bfloat16
    )
    d_gates = jnp.take(slot_dg, dest) * keep.astype(jnp.bfloat16)
    return (d_tokens, d_gates, dwg[None], dwu[None], dwd[None])


def paired(mesh):
    counts = (mesh.shape["ep"], mesh.shape["zr"])
    return all(c > 2 and c & (c - 1) == 0 for c in counts)


def tiled(mesh, tokens):
    n_experts, n_groups = mesh.shape["ep"], mesh.shape["zr"]
    capacity = 3 * (tokens.shape[0] // (n_experts * n_groups)) // n_experts
    return paired(mesh) and capacity % 16 == 0 and tokens.shape[1] % LANES == 0


def solution(mesh):
    placed = (
        P(("ep", "zr"), None),
        P(("ep", "zr"), None),
        P(("ep", "zr"), None),
        P(("ep", "zr"), None),
        P(("ep", "zr"), None),
        P("ep", None, "zr"),
        P("ep", None, "zr"),
        P("ep", "zr", None),
    )

    def sharded(local):
        return jax.shard_map(
            local,
            mesh=mesh,
            in_specs=placed,
            out_specs=(
                P(("ep", "zr"), None),
                P(("ep", "zr"), None),
                P("ep", None, "zr"),
                P("ep", None, "zr"),
                P("ep", "zr", None),
            ),
            check_vma=False,
        )

    def step(tokens, *rest):
        chosen = local_tiled if tiled(mesh, tokens) else local_general
        return sharded(chosen)(tokens, *rest)

    return step
```

profile of v0, /device:TPU:0, one launch (start us, length us, event | category | flops | bytes accessed | tf_op | source)
XLA Modules:
  0.0 124.7 jit_solution(16343729052772865226)
XLA Ops:
  0.7 1.0 copy-done.5
  1.7 0.9 copy-done.6
  2.6 0.7 copy-done.7
  3.3 0.7 copy-done.9
  4.0 0.7 copy-done.11
  4.6 0.8 shard_map.119
  5.4 3.1 %collective-permute-start = (bf16[96,1024]{1,0:T(8,128)(2,1)S(1)}, bf16[96,1024]{1,0:T(8,128)(2,1)S(1)}, u32[]{:S(2)}, u32[]{:S(2)}) collective-permute-start(bf16[96,1024]{1,0:T(8,128)(2,1)S(1)} %get-tuple-element.47), channel_id=1, source_target_pairs={{0,4},{4,0},{8,12},{12,8},{16,20},{20,16},{24,28},{28,24},{1,5},{5... | collective-permute-start | bytes 589832 | tf_op jit(solution)/shard_map/ppermute | solution.py:154
  8.5 2.6 %collective-permute-start.1 = (bf16[96,1024]{1,0:T(8,128)(2,1)S(1)}, bf16[96,1024]{1,0:T(8,128)(2,1)S(1)}, u32[]{:S(2)}, u32[]{:S(2)}) collective-permute-start(bf16[96,1024]{1,0:T(8,128)(2,1)S(1)} %get-tuple-element.48), channel_id=1, source_target_pairs={{0,16},{4,20},{8,24},{12,28},{16,0},{20,4},{24,8},{28,12},{1,17},{... | collective-permute-start | bytes 589832 | tf_op jit(solution)/shard_map/ppermute | solution.py:154
  11.1 1.6 %collective-permute-start.10 = (bf16[96,1024]{1,0:T(8,128)(2,1)S(1)}, bf16[96,1024]{1,0:T(8,128)(2,1)S(1)}, u32[]{:S(2)}, u32[]{:S(2)}) collective-permute-start(bf16[96,1024]{1,0:T(8,128)(2,1)S(1)} %get-tuple-element.53), channel_id=1, source_target_pairs={{0,8},{4,12},{8,0},{12,4},{16,24},{20,28},{24,16},{28,20},{1,9},{5... | collective-permute-start | bytes 589832 | tf_op jit(solution)/shard_map/ppermute | solution.py:154
  12.7 0.4 collective-permute-start.11
  13.1 1.3 %collective-permute-start.12 = (bf16[96,1024]{1,0:T(8,128)(2,1)S(1)}, bf16[96,1024]{1,0:T(8,128)(2,1)S(1)}, u32[]{:S(2)}, u32[]{:S(2)}) collective-permute-start(bf16[96,1024]{1,0:T(8,128)(2,1)S(1)} %get-tuple-element.55), channel_id=1, source_target_pairs={{0,20},{4,16},{8,28},{12,24},{16,4},{20,0},{24,12},{28,8},{1,21},{... | collective-permute-start | bytes 589832 | tf_op jit(solution)/shard_map/ppermute | solution.py:154
  14.4 0.0 collective-permute-done.refs_1_
  14.4 3.6 %collective-permute-start.21 = (bf16[96,1024]{1,0:T(8,128)(2,1)S(1)}, bf16[96,1024]{1,0:T(8,128)(2,1)S(1)}, u32[]{:S(2)}, u32[]{:S(2)}) collective-permute-start(bf16[96,1024]{1,0:T(8,128)(2,1)S(1)} %get-tuple-element.62), channel_id=1, source_target_pairs={{0,24},{4,28},{8,16},{12,20},{16,8},{20,12},{24,0},{28,4},{1,25},{... | collective-permute-start | bytes 589832 | tf_op jit(solution)/shard_map/ppermute | solution.py:154
  18.0 3.2 %collective-permute-done.1.refs_2_ = bf16[96,1024]{1,0:T(8,128)(2,1)S(1)} collective-permute-done((bf16[96,1024]{1,0:T(8,128)(2,1)S(1)}, bf16[96,1024]{1,0:T(8,128)(2,1)S(1)}, u32[]{:S(2)}, u32[]{:S(2)}) %collective-permute-start.1) | collective-permute-done | bytes 196640 | tf_op jit(solution)/shard_map/ppermute | solution.py:154
  21.2 4.8 %collective-permute-done.10.refs_0_.refs_6_ = bf16[96,1024]{1,0:T(8,128)(2,1)S(1)} collective-permute-done((bf16[96,1024]{1,0:T(8,128)(2,1)S(1)}, bf16[96,1024]{1,0:T(8,128)(2,1)S(1)}, u32[]{:S(2)}, u32[]{:S(2)}) %collective-permute-start.10) | collective-permute-done | bytes 196640 | tf_op jit(solution)/shard_map/ppermute | solution.py:154
  26.0 0.0 collective-permute-start.6
  26.0 3.1 %collective-permute-done.11.refs_1_.refs_7_ = bf16[96,1024]{1,0:T(8,128)(2,1)S(1)} collective-permute-done((bf16[96,1024]{1,0:T(8,128)(2,1)S(1)}, bf16[96,1024]{1,0:T(8,128)(2,1)S(1)}, u32[]{:S(2)}, u32[]{:S(2)}) %collective-permute-start.11) | collective-permute-done | bytes 196640 | tf_op jit(solution)/shard_map/ppermute | solution.py:154
  29.0 0.1 collective-permute-done.12.refs_2_.refs_8_
  29.1 3.5 %collective-permute-start.22 = (bf16[96,1024]{1,0:T(8,128)(2,1)S(1)}, bf16[96,1024]{1,0:T(8,128)(2,1)S(1)}, u32[]{:S(2)}, u32[]{:S(2)}) collective-permute-start(bf16[96,1024]{1,0:T(8,128)(2,1)S(1)} %get-tuple-element.63), channel_id=1, source_target_pairs={{0,28},{4,24},{8,20},{12,16},{16,12},{20,8},{24,4},{28,0},{1,29},{... | collective-permute-start | bytes 589832 | tf_op jit(solution)/shard_map/ppermute | solution.py:154
  32.6 1.2 collective-permute-done.21.refs_0_.refs_12_
  33.8 1.5 %collective-permute-start.2 = (bf16[96,1024]{1,0:T(8,128)(2,1)S(1)}, bf16[96,1024]{1,0:T(8,128)(2,1)S(1)}, u32[]{:S(2)}, u32[]{:S(2)}) collective-permute-start(bf16[96,1024]{1,0:T(8,128)(2,1)S(1)} %get-tuple-element.46.refs_0_), channel_id=1, source_target_pairs={{0,2},{1,3},{2,0},{3,1},{4,6},{5,7},{6,4},{7,5},{8,10},{9,11},{10,... | collective-permute-start | bytes 589832 | tf_op jit(solution)/shard_map/ppermute | solution.py:154
  35.3 3.9 %collective-permute-done.22.refs_1_.refs_13_ = bf16[96,1024]{1,0:T(8,128)(2,1)S(1)} collective-permute-done((bf16[96,1024]{1,0:T(8,128)(2,1)S(1)}, bf16[96,1024]{1,0:T(8,128)(2,1)S(1)}, u32[]{:S(2)}, u32[]{:S(2)}) %collective-permute-start.22) | collective-permute-done | bytes 196640 | tf_op jit(solution)/shard_map/ppermute | solution.py:154
  39.2 1.6 %collective-permute-start.3 = (bf16[96,1024]{1,0:T(8,128)(2,1)S(1)}, bf16[96,1024]{1,0:T(8,128)(2,1)S(1)}, u32[]{:S(2)}, u32[]{:S(2)}) collective-permute-start(bf16[96,1024]{1,0:T(8,128)(2,1)S(1)} %collective-permute-done.refs_1_), channel_id=1, source_target_pairs={{0,2},{1,3},{2,0},{3,1},{4,6},{5,7},{6,4},{7,5},{8,10},{9,11},{10,... | collective-permute-start | bytes 589832 | tf_op jit(solution)/shard_map/ppermute | solution.py:154
  40.8 0.0 collective-permute-done.2.refs_3_
  40.8 0.4 collective-permute-start.4
  41.2 5.7 %collective-permute-done.3.refs_4_ = bf16[96,1024]{1,0:T(8,128)(2,1)S(1)} collective-permute-done((bf16[96,1024]{1,0:T(8,128)(2,1)S(1)}, bf16[96,1024]{1,0:T(8,128)(2,1)S(1)}, u32[]{:S(2)}, u32[]{:S(2)}) %collective-permute-start.3) | collective-permute-done | bytes 196640 | tf_op jit(solution)/shard_map/ppermute | solution.py:154
  46.9 1.6 %collective-permute-start.23 = (bf16[96,1024]{1,0:T(8,128)(2,1)S(1)}, bf16[96,1024]{1,0:T(8,128)(2,1)S(1)}, u32[]{:S(2)}, u32[]{:S(2)}) collective-permute-start(bf16[96,1024]{1,0:T(8,128)(2,1)S(1)} %collective-permute-done.21.refs_0_.refs_12_), channel_id=1, source_target_pairs={{0,2},{1,3},{2,0},{3,1},{4,6},{5,7},{6,4},{7,5},{8,10},{9,11},{10,... | collective-permute-start | bytes 589832 | tf_op jit(solution)/shard_map/ppermute | solution.py:154
  48.5 2.6 %collective-permute-done.4.refs_5_ = bf16[96,1024]{1,0:T(8,128)(2,1)S(1)} collective-permute-done((bf16[96,1024]{1,0:T(8,128)(2,1)S(1)}, bf16[96,1024]{1,0:T(8,128)(2,1)S(1)}, u32[]{:S(2)}, u32[]{:S(2)}) %collective-permute-start.4) | collective-permute-done | bytes 196640 | tf_op jit(solution)/shard_map/ppermute | solution.py:154
  51.1 1.6 %collective-permute-start.24 = (bf16[96,1024]{1,0:T(8,128)(2,1)S(1)}, bf16[96,1024]{1,0:T(8,128)(2,1)S(1)}, u32[]{:S(2)}, u32[]{:S(2)}) collective-permute-start(bf16[96,1024]{1,0:T(8,128)(2,1)S(1)} %collective-permute-done.22.refs_1_.refs_13_), channel_id=1, source_target_pairs={{0,2},{1,3},{2,0},{3,1},{4,6},{5,7},{6,4},{7,5},{8,10},{9,11},{10,... | collective-permute-start | bytes 589832 | tf_op jit(solution)/shard_map/ppermute | solution.py:154
  52.8 0.4 collective-permute-start.13
  53.2 1.6 %collective-permute-start.14 = (bf16[96,1024]{1,0:T(8,128)(2,1)S(1)}, bf16[96,1024]{1,0:T(8,128)(2,1)S(1)}, u32[]{:S(2)}, u32[]{:S(2)}) collective-permute-start(bf16[96,1024]{1,0:T(8,128)(2,1)S(1)} %collective-permute-done.11.refs_1_.refs_7_), channel_id=1, source_target_pairs={{0,2},{1,3},{2,0},{3,1},{4,6},{5,7},{6,4},{7,5},{8,10},{9,11},{10,... | collective-permute-start | bytes 589832 | tf_op jit(solution)/shard_map/ppermute | solution.py:154
  54.8 0.4 collective-permute-start.15
  55.2 1.0 copy-done.1
  56.3 1.0 copy-done.3
  57.3 2.6 %shard_map.120 = (bf16[144,1152]{1,0:T(8,128)(2,1)S(1)}, bf16[144,1152]{1,0:T(8,128)(2,1)S(1)}, bf16[288,512]{1,0:T(8,128)(2,1)S(1)}, bf16[288,512]{1,0:T(8,128)(2,1)S(1)}, bf16[288,512]{1,0:T(8,128)(2,1)S(1)}) custom-call(bf16[96,1024]{1,0:T(8,128)(2,1)S(1)} %get-tuple-element.46.refs_0_, bf16[96,1024]{1,0:T(8,128)(2,1)S(1)} %collective-permute-done.refs_1_, ...), custom_call_target="tpu_custom_call" | custom-call | tf_op jit(solution)/shard_map/pallas_call | solution.py:157
  60.0 1.7 %collective-permute-start.8 = (bf16[144,1152]{1,0:T(8,128)(2,1)S(1)}, bf16[144,1152]{1,0:T(8,128)(2,1)S(1)}, u32[]{:S(2)}, u32[]{:S(2)}) collective-permute-start(bf16[144,1152]{1,0:T(8,128)(2,1)S(1)} %get-tuple-element.50), channel_id=1, source_target_pairs={{0,2},{1,3},{2,0},{3,1},{4,6},{5,7},{6,4},{7,5},{8,10},{9,11},{10,... | collective-permute-start | bytes 995336 | tf_op jit(solution)/shard_map/ppermute | solution.py:154
  61.6 2.1 %shard_map.124 = (bf16[96,1152]{1,0:T(8,128)(2,1)S(1)}, bf16[96,1152]{1,0:T(8,128)(2,1)S(1)}, bf16[192,512]{1,0:T(8,128)(2,1)S(1)}, bf16[192,512]{1,0:T(8,128)(2,1)S(1)}, bf16[192,512]{1,0:T(8,128)(2,1)S(1)}) custom-call(bf16[96,1024]{1,0:T(8,128)(2,1)S(1)} %collective-permute-done.21.refs_0_.refs_12_, ...), custom_call_target="tpu_custom_call" | custom-call | tf_op jit(solution)/shard_map/pallas_call | solution.py:157
  63.7 0.5 collective-permute-start.25
  64.2 3.8 %collective-permute-done.14.refs_4_.refs_10_ = bf16[96,1024]{1,0:T(8,128)(2,1)S(1)} collective-permute-done((bf16[96,1024]{1,0:T(8,128)(2,1)S(1)}, bf16[96,1024]{1,0:T(8,128)(2,1)S(1)}, u32[]{:S(2)}, u32[]{:S(2)}) %collective-permute-start.14) | collective-permute-done | bytes 196640 | tf_op jit(solution)/shard_map/ppermute | solution.py:154
  68.0 4.2 %collective-permute-done.15.refs_5_.refs_11_ = bf16[96,1024]{1,0:T(8,128)(2,1)S(1)} collective-permute-done((bf16[96,1024]{1,0:T(8,128)(2,1)S(1)}, bf16[96,1024]{1,0:T(8,128)(2,1)S(1)}, u32[]{:S(2)}, u32[]{:S(2)}) %collective-permute-start.15) | collective-permute-done | bytes 196640 | tf_op jit(solution)/shard_map/ppermute | solution.py:154
  72.2 2.6 %shard_map.122 = (bf16[144,1152]{1,0:T(8,128)(2,1)S(1)}, bf16[144,1152]{1,0:T(8,128)(2,1)S(1)}, bf16[288,512]{1,0:T(8,128)(2,1)S(1)}, bf16[288,512]{1,0:T(8,128)(2,1)S(1)}, bf16[288,512]{1,0:T(8,128)(2,1)S(1)}) custom-call(bf16[96,1024]{1,0:T(8,128)(2,1)S(1)} %collective-permute-done.10.refs_0_.refs_6_, ...), custom_call_target="tpu_custom_call" | custom-call | tf_op jit(solution)/shard_map/pallas_call | solution.py:157
  74.9 1.7 %collective-permute-start.16 = (bf16[144,1152]{1,0:T(8,128)(2,1)S(1)}, bf16[144,1152]{1,0:T(8,128)(2,1)S(1)}, u32[]{:S(2)}, u32[]{:S(2)}) collective-permute-start(bf16[144,1152]{1,0:T(8,128)(2,1)S(1)} %get-tuple-element.57), channel_id=1, source_target_pairs={{0,2},{1,3},{2,0},{3,1},{4,6},{5,7},{6,4},{7,5},{8,10},{9,11},{10,... | collective-permute-start | bytes 995336 | tf_op jit(solution)/shard_map/ppermute | solution.py:154
  76.5 1.4 %shard_map.127 = (bf16[1024,256]{1,0:T(8,128)(2,1)S(1)}, bf16[1024,256]{1,0:T(8,128)(2,1)S(1)}, bf16[256,1024]{1,0:T(8,128)(2,1)S(1)}) custom-call(bf16[96,1024]{1,0:T(8,128)(2,1)S(1)} %get-tuple-element.46.refs_0_, bf16[96,1024]{1,0:T(8,128)(2,1)S(1)} %collective-permute-done.refs_1_, bf16[96,1024]{1,0:T(8,128)(2,1)S(1)} %collective-permute-done.1.refs_2_, ...), custom_call_target="tpu_custom_call" | custom-call | tf_op jit(solution)/shard_map/pallas_call | solution.py:157
  78.0 0.1 collective-permute-start.28
  78.0 0.5 collective-permute-start.29
  78.5 5.5 %collective-permute-done.25.refs_1_ = bf16[96,1152]{1,0:T(8,128)(2,1)S(1)} collective-permute-done((bf16[96,1152]{1,0:T(8,128)(2,1)S(1)}, bf16[96,1152]{1,0:T(8,128)(2,1)S(1)}, u32[]{:S(2)}, u32[]{:S(2)}) %collective-permute-start.25) | collective-permute-done | bytes 221216 | tf_op jit(solution)/shard_map/ppermute | solution.py:154
  84.1 0.1 shard_map.125
  84.1 2.7 %collective-permute-start.26 = (bf16[48,1152]{1,0:T(8,128)(2,1)S(1)}, bf16[48,1152]{1,0:T(8,128)(2,1)S(1)}, u32[]{:S(2)}, u32[]{:S(2)}) collective-permute-start(bf16[48,1152]{1,0:T(8,128)(2,1)S(1)} %get-tuple-element.66), channel_id=1, source_target_pairs={{0,24},{4,28},{8,16},{12,20},{16,8},{20,12},{24,0},{28,4},{1,25},{... | collective-permute-start | bytes 331784 | tf_op jit(solution)/shard_map/ppermute | solution.py:154
  86.8 0.1 shard_map.121
  86.9 4.6 %collective-permute-done.26.refs_6_ = bf16[48,1152]{1,0:T(8,128)(2,1)S(1)} collective-permute-done((bf16[48,1152]{1,0:T(8,128)(2,1)S(1)}, bf16[48,1152]{1,0:T(8,128)(2,1)S(1)}, u32[]{:S(2)}, u32[]{:S(2)}) %collective-permute-start.26) | collective-permute-done | bytes 110624 | tf_op jit(solution)/shard_map/ppermute | solution.py:154
  91.5 3.6 %collective-permute-start.27 = (bf16[48,1152]{1,0:T(8,128)(2,1)S(1)}, bf16[48,1152]{1,0:T(8,128)(2,1)S(1)}, u32[]{:S(2)}, u32[]{:S(2)}) collective-permute-start(bf16[48,1152]{1,0:T(8,128)(2,1)S(1)} %get-tuple-element.67), channel_id=1, source_target_pairs={{0,28},{4,24},{8,20},{12,16},{16,12},{20,8},{24,4},{28,0},{1,29},{... | collective-permute-start | bytes 331784 | tf_op jit(solution)/shard_map/ppermute | solution.py:154
  95.0 0.5 collective-permute-start.9
  95.5 0.1 shard_map.123
  95.6 3.3 %collective-permute-done.27.refs_7_ = bf16[48,1152]{1,0:T(8,128)(2,1)S(1)} collective-permute-done((bf16[48,1152]{1,0:T(8,128)(2,1)S(1)}, bf16[48,1152]{1,0:T(8,128)(2,1)S(1)}, u32[]{:S(2)}, u32[]{:S(2)}) %collective-permute-start.27) | collective-permute-done | bytes 110624 | tf_op jit(solution)/shard_map/ppermute | solution.py:154
  99.0 7.5 %collective-permute-start.19 = (bf16[48,1152]{1,0:T(8,128)(2,1)S(1)}, bf16[48,1152]{1,0:T(8,128)(2,1)S(1)}, u32[]{:S(2)}, u32[]{:S(2)}) collective-permute-start(bf16[48,1152]{1,0:T(8,128)(2,1)S(1)} %get-tuple-element.60), channel_id=1, source_target_pairs={{0,16},{4,20},{8,24},{12,28},{16,0},{20,4},{24,8},{28,12},{1,17},{... | collective-permute-start | bytes 331784 | tf_op jit(solution)/shard_map/ppermute | solution.py:154
  106.5 1.0 collective-permute-start.17
  107.5 2.4 %collective-permute-done.19.refs_4_ = bf16[48,1152]{1,0:T(8,128)(2,1)S(1)} collective-permute-done((bf16[48,1152]{1,0:T(8,128)(2,1)S(1)}, bf16[48,1152]{1,0:T(8,128)(2,1)S(1)}, u32[]{:S(2)}, u32[]{:S(2)}) %collective-permute-start.19) | collective-permute-done | bytes 110624 | tf_op jit(solution)/shard_map/ppermute | solution.py:154
  109.9 3.6 %collective-permute-start.18 = (bf16[48,1152]{1,0:T(8,128)(2,1)S(1)}, bf16[48,1152]{1,0:T(8,128)(2,1)S(1)}, u32[]{:S(2)}, u32[]{:S(2)}) collective-permute-start(bf16[48,1152]{1,0:T(8,128)(2,1)S(1)} %get-tuple-element.59), channel_id=1, source_target_pairs={{0,12},{4,8},{8,4},{12,0},{16,28},{20,24},{24,20},{28,16},{1,13},{... | collective-permute-start | bytes 331784 | tf_op jit(solution)/shard_map/ppermute | solution.py:154
  113.4 1.7 %collective-permute-start.20 = (bf16[48,1152]{1,0:T(8,128)(2,1)S(1)}, bf16[48,1152]{1,0:T(8,128)(2,1)S(1)}, u32[]{:S(2)}, u32[]{:S(2)}) collective-permute-start(bf16[48,1152]{1,0:T(8,128)(2,1)S(1)} %get-tuple-element.61), channel_id=1, source_target_pairs={{0,20},{4,16},{8,28},{12,24},{16,4},{20,0},{24,12},{28,8},{1,21},{... | collective-permute-start | bytes 331784 | tf_op jit(solution)/shard_map/ppermute | solution.py:154
  115.1 1.4 %collective-permute-done.18.refs_3_ = bf16[48,1152]{1,0:T(8,128)(2,1)S(1)} collective-permute-done((bf16[48,1152]{1,0:T(8,128)(2,1)S(1)}, bf16[48,1152]{1,0:T(8,128)(2,1)S(1)}, u32[]{:S(2)}, u32[]{:S(2)}) %collective-permute-start.18) | collective-permute-done | bytes 110624 | tf_op jit(solution)/shard_map/ppermute | solution.py:154
  116.5 4.2 %collective-permute-done.20.refs_5_ = bf16[48,1152]{1,0:T(8,128)(2,1)S(1)} collective-permute-done((bf16[48,1152]{1,0:T(8,128)(2,1)S(1)}, bf16[48,1152]{1,0:T(8,128)(2,1)S(1)}, u32[]{:S(2)}, u32[]{:S(2)}) %collective-permute-start.20) | collective-permute-done | bytes 110624 | tf_op jit(solution)/shard_map/ppermute | solution.py:154
  120.7 0.7 copy-done.8
  121.4 1.0 shard_map.126
  122.5 2.3 %shard_map.128 = (bf16[1024,256]{1,0:T(8,128)(2,1)}, bf16[1024,256]{1,0:T(8,128)(2,1)}, bf16[256,1024]{1,0:T(8,128)(2,1)}) custom-call(bf16[96,1024]{1,0:T(8,128)(2,1)S(1)} %get-tuple-element.46.refs_0_, bf16[96,1024]{1,0:T(8,128)(2,1)S(1)} %collective-permute-done.refs_1_, bf16[96,1024]{1,0:T(8,128)(2,1)S(1)} %collective-permute-done.1.refs_2_, ...), custom_call_target="tpu_custom_call" | custom-call | tf_op jit(solution)/shard_map/pallas_call | solution.py:157
  (34 shorter events, 0.1 us)
Async XLA Ops:
  0.6 20.6 %copy-start = (bf16[1,1024,256]{2,1,0:T(8,128)(2,1)S(1)}, bf16[1,1024,256]{2,1,0:T(8,128)(2,1)}, u32[]{:S(2)}) copy-start(bf16[1,1024,256]{2,1,0:T(8,128)(2,1)} %param.13) | copy-start | bytes 1572868
  0.6 1.0 copy-start.5
  1.7 0.9 copy-start.6
  2.6 0.7 copy-start.7
  3.3 0.7 copy-start.9
  4.0 0.7 copy-start.11
  5.4 8.9 %collective-permute-start = (bf16[96,1024]{1,0:T(8,128)(2,1)S(1)}, bf16[96,1024]{1,0:T(8,128)(2,1)S(1)}, u32[]{:S(2)}, u32[]{:S(2)}) collective-permute-start(bf16[96,1024]{1,0:T(8,128)(2,1)S(1)} %get-tuple-element.47), channel_id=1, source_target_pairs={{0,4},{4,0},{8,12},{12,8},{16,20},{20,16},{24,28},{28,24},{1,5},{5... | collective-permute-start | bytes 589832 | tf_op jit(solution)/shard_map/ppermute | solution.py:154
  8.5 12.7 %collective-permute-start.1 = (bf16[96,1024]{1,0:T(8,128)(2,1)S(1)}, bf16[96,1024]{1,0:T(8,128)(2,1)S(1)}, u32[]{:S(2)}, u32[]{:S(2)}) collective-permute-start(bf16[96,1024]{1,0:T(8,128)(2,1)S(1)} %get-tuple-element.48), channel_id=1, source_target_pairs={{0,16},{4,20},{8,24},{12,28},{16,0},{20,4},{24,8},{28,12},{1,17},{... | collective-permute-start | bytes 589832 | tf_op jit(solution)/shard_map/ppermute | solution.py:154
  11.1 14.9 %collective-permute-start.10 = (bf16[96,1024]{1,0:T(8,128)(2,1)S(1)}, bf16[96,1024]{1,0:T(8,128)(2,1)S(1)}, u32[]{:S(2)}, u32[]{:S(2)}) collective-permute-start(bf16[96,1024]{1,0:T(8,128)(2,1)S(1)} %get-tuple-element.53), channel_id=1, source_target_pairs={{0,8},{4,12},{8,0},{12,4},{16,24},{20,28},{24,16},{28,20},{1,9},{5... | collective-permute-start | bytes 589832 | tf_op jit(solution)/shard_map/ppermute | solution.py:154
  12.7 16.4 %collective-permute-start.11 = (bf16[96,1024]{1,0:T(8,128)(2,1)S(1)}, bf16[96,1024]{1,0:T(8,128)(2,1)S(1)}, u32[]{:S(2)}, u32[]{:S(2)}) collective-permute-start(bf16[96,1024]{1,0:T(8,128)(2,1)S(1)} %get-tuple-element.54), channel_id=1, source_target_pairs={{0,12},{4,8},{8,4},{12,0},{16,28},{20,24},{24,20},{28,16},{1,13},{... | collective-permute-start | bytes 589832 | tf_op jit(solution)/shard_map/ppermute | solution.py:154
  13.1 16.0 %collective-permute-start.12 = (bf16[96,1024]{1,0:T(8,128)(2,1)S(1)}, bf16[96,1024]{1,0:T(8,128)(2,1)S(1)}, u32[]{:S(2)}, u32[]{:S(2)}) collective-permute-start(bf16[96,1024]{1,0:T(8,128)(2,1)S(1)} %get-tuple-element.55), channel_id=1, source_target_pairs={{0,20},{4,16},{8,28},{12,24},{16,4},{20,0},{24,12},{28,8},{1,21},{... | collective-permute-start | bytes 589832 | tf_op jit(solution)/shard_map/ppermute | solution.py:154
  14.4 19.4 %collective-permute-start.21 = (bf16[96,1024]{1,0:T(8,128)(2,1)S(1)}, bf16[96,1024]{1,0:T(8,128)(2,1)S(1)}, u32[]{:S(2)}, u32[]{:S(2)}) collective-permute-start(bf16[96,1024]{1,0:T(8,128)(2,1)S(1)} %get-tuple-element.62), channel_id=1, source_target_pairs={{0,24},{4,28},{8,16},{12,20},{16,8},{20,12},{24,0},{28,4},{1,25},{... | collective-permute-start | bytes 589832 | tf_op jit(solution)/shard_map/ppermute | solution.py:154
  21.2 31.6 %collective-permute-start.5 = (bf16[1024,256]{1,0:T(8,128)(2,1)S(1)}, bf16[1024,256]{1,0:T(8,128)(2,1)S(1)}, u32[]{:S(2)}, u32[]{:S(2)}) collective-permute-start(bf16[1024,256]{1,0:T(8,128)(2,1)S(1)} %bitcast.11), channel_id=1, source_target_pairs={{0,1},{1,0},{2,3},{3,2},{4,5},{5,4},{6,7},{7,6},{8,9},{9,8},{10,11... | collective-permute-start | bytes 1572872 | tf_op jit(solution)/shard_map/ppermute | solution.py:154
  26.0 27.2 %collective-permute-start.6 = (bf16[1024,256]{1,0:T(8,128)(2,1)}, bf16[1024,256]{1,0:T(8,128)(2,1)S(1)}, u32[]{:S(2)}, u32[]{:S(2)}) collective-permute-start(bf16[1024,256]{1,0:T(8,128)(2,1)} %bitcast.15), channel_id=1, source_target_pairs={{0,1},{1,0},{2,3},{3,2},{4,5},{5,4},{6,7},{7,6},{8,9},{9,8},{10,11... | collective-permute-start | bytes 1572872 | tf_op jit(solution)/shard_map/ppermute | solution.py:154
  29.0 25.8 %collective-permute-start.7 = (bf16[256,1024]{1,0:T(8,128)(2,1)}, bf16[256,1024]{1,0:T(8,128)(2,1)S(1)}, u32[]{:S(2)}, u32[]{:S(2)}) collective-permute-start(bf16[256,1024]{1,0:T(8,128)(2,1)} %bitcast.19), channel_id=1, source_target_pairs={{0,1},{1,0},{2,3},{3,2},{4,5},{5,4},{6,7},{7,6},{8,9},{9,8},{10,11... | collective-permute-start | bytes 1572872 | tf_op jit(solution)/shard_map/ppermute | solution.py:154
  29.1 10.0 %collective-permute-start.22 = (bf16[96,1024]{1,0:T(8,128)(2,1)S(1)}, bf16[96,1024]{1,0:T(8,128)(2,1)S(1)}, u32[]{:S(2)}, u32[]{:S(2)}) collective-permute-start(bf16[96,1024]{1,0:T(8,128)(2,1)S(1)} %get-tuple-element.63), channel_id=1, source_target_pairs={{0,28},{4,24},{8,20},{12,16},{16,12},{20,8},{24,4},{28,0},{1,29},{... | collective-permute-start | bytes 589832 | tf_op jit(solution)/shard_map/ppermute | solution.py:154
  33.8 7.0 %collective-permute-start.2 = (bf16[96,1024]{1,0:T(8,128)(2,1)S(1)}, bf16[96,1024]{1,0:T(8,128)(2,1)S(1)}, u32[]{:S(2)}, u32[]{:S(2)}) collective-permute-start(bf16[96,1024]{1,0:T(8,128)(2,1)S(1)} %get-tuple-element.46.refs_0_), channel_id=1, source_target_pairs={{0,2},{1,3},{2,0},{3,1},{4,6},{5,7},{6,4},{7,5},{8,10},{9,11},{10,... | collective-permute-start | bytes 589832 | tf_op jit(solution)/shard_map/ppermute | solution.py:154
  39.2 7.8 %collective-permute-start.3 = (bf16[96,1024]{1,0:T(8,128)(2,1)S(1)}, bf16[96,1024]{1,0:T(8,128)(2,1)S(1)}, u32[]{:S(2)}, u32[]{:S(2)}) collective-permute-start(bf16[96,1024]{1,0:T(8,128)(2,1)S(1)} %collective-permute-done.refs_1_), channel_id=1, source_target_pairs={{0,2},{1,3},{2,0},{3,1},{4,6},{5,7},{6,4},{7,5},{8,10},{9,11},{10,... | collective-permute-start | bytes 589832 | tf_op jit(solution)/shard_map/ppermute | solution.py:154
  40.8 10.4 %collective-permute-start.4 = (bf16[96,1024]{1,0:T(8,128)(2,1)S(1)}, bf16[96,1024]{1,0:T(8,128)(2,1)S(1)}, u32[]{:S(2)}, u32[]{:S(2)}) collective-permute-start(bf16[96,1024]{1,0:T(8,128)(2,1)S(1)} %collective-permute-done.1.refs_2_), channel_id=1, source_target_pairs={{0,2},{1,3},{2,0},{3,1},{4,6},{5,7},{6,4},{7,5},{8,10},{9,11},{10,... | collective-permute-start | bytes 589832 | tf_op jit(solution)/shard_map/ppermute | solution.py:154
  46.9 13.0 %collective-permute-start.23 = (bf16[96,1024]{1,0:T(8,128)(2,1)S(1)}, bf16[96,1024]{1,0:T(8,128)(2,1)S(1)}, u32[]{:S(2)}, u32[]{:S(2)}) collective-permute-start(bf16[96,1024]{1,0:T(8,128)(2,1)S(1)} %collective-permute-done.21.refs_0_.refs_12_), channel_id=1, source_target_pairs={{0,2},{1,3},{2,0},{3,1},{4,6},{5,7},{6,4},{7,5},{8,10},{9,11},{10,... | collective-permute-start | bytes 589832 | tf_op jit(solution)/shard_map/ppermute | solution.py:154
  51.1 10.5 %collective-permute-start.24 = (bf16[96,1024]{1,0:T(8,128)(2,1)S(1)}, bf16[96,1024]{1,0:T(8,128)(2,1)S(1)}, u32[]{:S(2)}, u32[]{:S(2)}) collective-permute-start(bf16[96,1024]{1,0:T(8,128)(2,1)S(1)} %collective-permute-done.22.refs_1_.refs_13_), channel_id=1, source_target_pairs={{0,2},{1,3},{2,0},{3,1},{4,6},{5,7},{6,4},{7,5},{8,10},{9,11},{10,... | collective-permute-start | bytes 589832 | tf_op jit(solution)/shard_map/ppermute | solution.py:154
  52.8 11.4 %collective-permute-start.13 = (bf16[96,1024]{1,0:T(8,128)(2,1)S(1)}, bf16[96,1024]{1,0:T(8,128)(2,1)S(1)}, u32[]{:S(2)}, u32[]{:S(2)}) collective-permute-start(bf16[96,1024]{1,0:T(8,128)(2,1)S(1)} %collective-permute-done.10.refs_0_.refs_6_), channel_id=1, source_target_pairs={{0,2},{1,3},{2,0},{3,1},{4,6},{5,7},{6,4},{7,5},{8,10},{9,11},{10,... | collective-permute-start | bytes 589832 | tf_op jit(solution)/shard_map/ppermute | solution.py:154
  53.2 14.8 %collective-permute-start.14 = (bf16[96,1024]{1,0:T(8,128)(2,1)S(1)}, bf16[96,1024]{1,0:T(8,128)(2,1)S(1)}, u32[]{:S(2)}, u32[]{:S(2)}) collective-permute-start(bf16[96,1024]{1,0:T(8,128)(2,1)S(1)} %collective-permute-done.11.refs_1_.refs_7_), channel_id=1, source_target_pairs={{0,2},{1,3},{2,0},{3,1},{4,6},{5,7},{6,4},{7,5},{8,10},{9,11},{10,... | collective-permute-start | bytes 589832 | tf_op jit(solution)/shard_map/ppermute | solution.py:154
  54.8 17.4 %collective-permute-start.15 = (bf16[96,1024]{1,0:T(8,128)(2,1)S(1)}, bf16[96,1024]{1,0:T(8,128)(2,1)S(1)}, u32[]{:S(2)}, u32[]{:S(2)}) collective-permute-start(bf16[96,1024]{1,0:T(8,128)(2,1)S(1)} %collective-permute-done.12.refs_2_.refs_8_), channel_id=1, source_target_pairs={{0,2},{1,3},{2,0},{3,1},{4,6},{5,7},{6,4},{7,5},{8,10},{9,11},{10,... | collective-permute-start | bytes 589832 | tf_op jit(solution)/shard_map/ppermute | solution.py:154
  55.2 1.0 copy-start.1
  56.3 1.0 copy-start.3
  57.3 4.3 %copy-start.2 = (bf16[1,1024,256]{2,1,0:T(8,128)(2,1)S(1)}, bf16[1,1024,256]{2,1,0:T(8,128)(2,1)}, u32[]{:S(2)}) copy-start(bf16[1,1024,256]{2,1,0:T(8,128)(2,1)} %param.14) | copy-start | bytes 1572868
  57.3 4.3 %copy-start.4 = (bf16[1,256,1024]{2,1,0:T(8,128)(2,1)S(1)}, bf16[1,256,1024]{2,1,0:T(8,128)(2,1)}, u32[]{:S(2)}) copy-start(bf16[1,256,1024]{2,1,0:T(8,128)(2,1)} %param.15) | copy-start | bytes 1572868
  60.0 24.2 %collective-permute-start.8 = (bf16[144,1152]{1,0:T(8,128)(2,1)S(1)}, bf16[144,1152]{1,0:T(8,128)(2,1)S(1)}, u32[]{:S(2)}, u32[]{:S(2)}) collective-permute-start(bf16[144,1152]{1,0:T(8,128)(2,1)S(1)} %get-tuple-element.50), channel_id=1, source_target_pairs={{0,2},{1,3},{2,0},{3,1},{4,6},{5,7},{6,4},{7,5},{8,10},{9,11},{10,... | collective-permute-start | bytes 995336 | tf_op jit(solution)/shard_map/ppermute | solution.py:154
  63.7 20.4 %collective-permute-start.25 = (bf16[96,1152]{1,0:T(8,128)(2,1)S(1)}, bf16[96,1152]{1,0:T(8,128)(2,1)S(1)}, u32[]{:S(2)}, u32[]{:S(2)}) collective-permute-start(bf16[96,1152]{1,0:T(8,128)(2,1)S(1)} %get-tuple-element.65), channel_id=1, source_target_pairs={{0,2},{1,3},{2,0},{3,1},{4,6},{5,7},{6,4},{7,5},{8,10},{9,11},{10,... | collective-permute-start | bytes 663560 | tf_op jit(solution)/shard_map/ppermute | solution.py:154
  74.9 20.2 %collective-permute-start.16 = (bf16[144,1152]{1,0:T(8,128)(2,1)S(1)}, bf16[144,1152]{1,0:T(8,128)(2,1)S(1)}, u32[]{:S(2)}, u32[]{:S(2)}) collective-permute-start(bf16[144,1152]{1,0:T(8,128)(2,1)S(1)} %get-tuple-element.57), channel_id=1, source_target_pairs={{0,2},{1,3},{2,0},{3,1},{4,6},{5,7},{6,4},{7,5},{8,10},{9,11},{10,... | collective-permute-start | bytes 995336 | tf_op jit(solution)/shard_map/ppermute | solution.py:154
  78.0 44.5 %collective-permute-start.28 = (bf16[1024,256]{1,0:T(8,128)(2,1)S(1)}, bf16[1024,256]{1,0:T(8,128)(2,1)S(1)}, u32[]{:S(2)}, u32[]{:S(2)}) collective-permute-start(bf16[1024,256]{1,0:T(8,128)(2,1)S(1)} %get-tuple-element.79), channel_id=1, source_target_pairs={{0,1},{1,0},{2,3},{3,2},{4,5},{5,4},{6,7},{7,6},{8,9},{9,8},{10,11... | collective-permute-start | bytes 1572872 | tf_op jit(solution)/shard_map/ppermute | solution.py:154
  78.0 44.4 %collective-permute-start.29 = (bf16[1024,256]{1,0:T(8,128)(2,1)S(1)}, bf16[1024,256]{1,0:T(8,128)(2,1)S(1)}, u32[]{:S(2)}, u32[]{:S(2)}) collective-permute-start(bf16[1024,256]{1,0:T(8,128)(2,1)S(1)} %get-tuple-element.80), channel_id=1, source_target_pairs={{0,1},{1,0},{2,3},{3,2},{4,5},{5,4},{6,7},{7,6},{8,9},{9,8},{10,11... | collective-permute-start | bytes 1572872 | tf_op jit(solution)/shard_map/ppermute | solution.py:154
  84.1 38.4 %collective-permute-start.30 = (bf16[256,1024]{1,0:T(8,128)(2,1)S(1)}, bf16[256,1024]{1,0:T(8,128)(2,1)S(1)}, u32[]{:S(2)}, u32[]{:S(2)}) collective-permute-start(bf16[256,1024]{1,0:T(8,128)(2,1)S(1)} %get-tuple-element.81), channel_id=1, source_target_pairs={{0,1},{1,0},{2,3},{3,2},{4,5},{5,4},{6,7},{7,6},{8,9},{9,8},{10,11... | collective-permute-start | bytes 1572872 | tf_op jit(solution)/shard_map/ppermute | solution.py:154
  84.1 7.3 %collective-permute-start.26 = (bf16[48,1152]{1,0:T(8,128)(2,1)S(1)}, bf16[48,1152]{1,0:T(8,128)(2,1)S(1)}, u32[]{:S(2)}, u32[]{:S(2)}) collective-permute-start(bf16[48,1152]{1,0:T(8,128)(2,1)S(1)} %get-tuple-element.66), channel_id=1, source_target_pairs={{0,24},{4,28},{8,16},{12,20},{16,8},{20,12},{24,0},{28,4},{1,25},{... | collective-permute-start | bytes 331784 | tf_op jit(solution)/shard_map/ppermute | solution.py:154
  91.5 7.5 %collective-permute-start.27 = (bf16[48,1152]{1,0:T(8,128)(2,1)S(1)}, bf16[48,1152]{1,0:T(8,128)(2,1)S(1)}, u32[]{:S(2)}, u32[]{:S(2)}) collective-permute-start(bf16[48,1152]{1,0:T(8,128)(2,1)S(1)} %get-tuple-element.67), channel_id=1, source_target_pairs={{0,28},{4,24},{8,20},{12,16},{16,12},{20,8},{24,4},{28,0},{1,29},{... | collective-permute-start | bytes 331784 | tf_op jit(solution)/shard_map/ppermute | solution.py:154
  95.0 11.4 %collective-permute-start.9 = (bf16[48,1152]{1,0:T(8,128)(2,1)S(1)}, bf16[48,1152]{1,0:T(8,128)(2,1)S(1)}, u32[]{:S(2)}, u32[]{:S(2)}) collective-permute-start(bf16[48,1152]{1,0:T(8,128)(2,1)S(1)} %get-tuple-element.52), channel_id=1, source_target_pairs={{0,4},{4,0},{8,12},{12,8},{16,20},{20,16},{24,28},{28,24},{1,5},{5... | collective-permute-start | bytes 331784 | tf_op jit(solution)/shard_map/ppermute | solution.py:154
  95.5 25.2 %copy-start.10 = (s32[128,2]{0,1:T(2,128)S(1)}, s32[128,2]{0,1:T(2,128)}, u32[]{:S(2)}) copy-start(s32[128,2]{0,1:T(2,128)} %param.12) | copy-start | bytes 3076
  99.0 10.9 %collective-permute-start.19 = (bf16[48,1152]{1,0:T(8,128)(2,1)S(1)}, bf16[48,1152]{1,0:T(8,128)(2,1)S(1)}, u32[]{:S(2)}, u32[]{:S(2)}) collective-permute-start(bf16[48,1152]{1,0:T(8,128)(2,1)S(1)} %get-tuple-element.60), channel_id=1, source_target_pairs={{0,16},{4,20},{8,24},{12,28},{16,0},{20,4},{24,8},{28,12},{1,17},{... | collective-permute-start | bytes 331784 | tf_op jit(solution)/shard_map/ppermute | solution.py:154
  106.5 7.0 %collective-permute-start.17 = (bf16[48,1152]{1,0:T(8,128)(2,1)S(1)}, bf16[48,1152]{1,0:T(8,128)(2,1)S(1)}, u32[]{:S(2)}, u32[]{:S(2)}) collective-permute-start(bf16[48,1152]{1,0:T(8,128)(2,1)S(1)} %get-tuple-element.58), channel_id=1, source_target_pairs={{0,8},{4,12},{8,0},{12,4},{16,24},{20,28},{24,16},{28,20},{1,9},{5... | collective-permute-start | bytes 331784 | tf_op jit(solution)/shard_map/ppermute | solution.py:154
  109.9 6.7 %collective-permute-start.18 = (bf16[48,1152]{1,0:T(8,128)(2,1)S(1)}, bf16[48,1152]{1,0:T(8,128)(2,1)S(1)}, u32[]{:S(2)}, u32[]{:S(2)}) collective-permute-start(bf16[48,1152]{1,0:T(8,128)(2,1)S(1)} %get-tuple-element.59), channel_id=1, source_target_pairs={{0,12},{4,8},{8,4},{12,0},{16,28},{20,24},{24,20},{28,16},{1,13},{... | collective-permute-start | bytes 331784 | tf_op jit(solution)/shard_map/ppermute | solution.py:154
  113.4 7.3 %collective-permute-start.20 = (bf16[48,1152]{1,0:T(8,128)(2,1)S(1)}, bf16[48,1152]{1,0:T(8,128)(2,1)S(1)}, u32[]{:S(2)}, u32[]{:S(2)}) collective-permute-start(bf16[48,1152]{1,0:T(8,128)(2,1)S(1)} %get-tuple-element.61), channel_id=1, source_target_pairs={{0,20},{4,16},{8,28},{12,24},{16,4},{20,0},{24,12},{28,8},{1,21},{... | collective-permute-start | bytes 331784 | tf_op jit(solution)/shard_map/ppermute | solution.py:154
  120.7 0.7 copy-start.8
  120.7 0.7 copy-start.12
where the time goes:
time: 125 us
  waiting for transfers between devices  54 us (43%)
  starting transfers between devices  50.1 us (40%)
  Pallas kernels  13.1 us (10%)
  local copies, waits for them, and re-layouts  6.74 us (5%)
    ppermute x31, waiting for transfers between devices, exchange(): return lax.ppermute(value, axis, [(i, i ^ bit) for i in range(size)])  54 us
    ppermute x31, starting transfers between devices, exchange(): return lax.ppermute(value, axis, [(i, i ^ bit) for i in range(size)])  50.1 us
    pallas_call x10, Pallas kernels, run(): return call(body, outs, len(args), smem=smem)(*args)  13.1 us
    unnamed x26, local copies, waits for them, and re-layouts  6.74 us
  transfers between devices with their start and end apart: 31, of which 16 were waited for; matrix products, arithmetic and copies ran while one was open for 0% of the time, Pallas kernels for 8%

commit v1 on v0

--- a/solution.py
+++ b/solution.py
@@ -11,6 +11,7 @@
 F32 = jnp.float32
 BF16 = jnp.bfloat16
 LANES = 128
+SUBLANES = 8
 VMEM_LIMIT = 24 * 1024 * 1024
 
 
@@ -18,12 +19,28 @@
     return lax.dot_general(a, b, (((dim_a,), (dim_b,)), ((), ())), preferred_element_type=F32)
 
 
-def send_kernel(n_experts, capacity, me_ref, exp_ref, keep_ref, gate_ref, tok_ref, cot_ref, *outs):
+def fetch(sources, targets, sems):
+    copies = [pltpu.make_async_copy(a, b, sems.at[i]) for i, (a, b) in enumerate(zip(sources, targets))]
+    for copy in copies:
+        copy.start()
+    return copies
+
+
+def send_kernel(n_experts, capacity, me_ref, *refs):
+    sources, refs = refs[:5], refs[5:]
+    (table_ref, exp_out, ratio_out), refs = refs[:3], refs[3:]
+    messages, (exp_ref, keep_ref, gate_ref, tok_ref, cot_ref, sems) = refs[:n_experts], refs[n_experts:]
+    copies = fetch(sources, (exp_ref, keep_ref, gate_ref, tok_ref, cot_ref), sems)
     rows = tok_ref.shape[0]
-    table_ref, messages = outs[0], outs[1:]
     earlier = lax.broadcasted_iota(jnp.int32, (rows, rows), 0) < lax.broadcasted_iota(jnp.int32, (rows, rows), 1)
-    weight = gate_ref[...].astype(F32) * keep_ref[...].astype(F32)
     ids = lax.broadcasted_iota(jnp.int32, (n_experts, rows), 0) ^ me_ref[0]
+    for copy in copies[:3]:
+        copy.wait()
+    gate = gate_ref[...].astype(F32)
+    keep = keep_ref[...].astype(F32)
+    weight = gate * keep
+    exp_out[...] = exp_ref[...]
+    ratio_out[...] = keep / gate
     named0 = exp_ref[0:1, :] == ids
     named1 = exp_ref[1:2, :] == ids
     named = named0 | named1
@@ -31,6 +48,8 @@
     position = contract(jnp.where(named, 1.0, 0.0).astype(BF16), jnp.where(earlier, 1.0, 0.0).astype(BF16), 1, 0)
     position = jnp.where(named, position, -1.0)
     slots = lax.broadcasted_iota(jnp.int32, (capacity, rows), 0).astype(F32)
+    for copy in copies[3:]:
+        copy.wait()
     for k in range(n_experts):
         hit = slots == position[k : k + 1, :]
         table = jnp.where(hit, 1.0, 0.0).astype(BF16)
@@ -40,12 +59,28 @@
         messages[k][capacity:, :] = contract(table_w, cot_ref[...], 1, 0).astype(BF16)
 
 
-def grad_kernel(n_msgs, n_own, capacity, *refs):
+def stage_kernel(*refs):
+    for copy in fetch(refs[:3], refs[3:6], refs[6]):
+        copy.wait()
+
+
+def pack(target, m, capacity, values, sums):
+    blocks = values.shape[1] // LANES
+    base = m * (blocks * capacity + SUBLANES)
+    for j in range(blocks):
+        target[base + j * capacity : base + (j + 1) * capacity, :] = values[:, j * LANES : (j + 1) * LANES].astype(BF16)
+    tail = slice(base + blocks * capacity, base + blocks * capacity + SUBLANES)
+    target[tail, :] = jnp.zeros((SUBLANES, LANES), BF16)
+    target[tail, 0:capacity] = sums.astype(BF16)
+
+
+def grad_kernel(n_parts, chunks, capacity, *refs):
+    n_own = sum(chunks)
+    n_msgs = n_parts * n_own
     msgs = refs[:n_msgs]
     wg_refs, wu_refs, wd_refs = refs[n_msgs : n_msgs + 2], refs[n_msgs + 2 : n_msgs + 4], refs[n_msgs + 4 : n_msgs + 6]
     outs = refs[n_msgs + 6 :]
     back, (da_ref, db_ref, h_ref) = outs[:-3], outs[-3:]
-    width = msgs[0].shape[1]
     x = jnp.concatenate([m[0:capacity, :] for m in msgs], axis=0)
     gw = jnp.concatenate([m[capacity:, :] for m in msgs], axis=0)
     part_x = None
@@ -65,23 +100,28 @@
         db_ref[:, cols] = db
         h_ref[:, cols] = h.astype(BF16)
         px = contract(da, wg_refs[q][...], 1, 1) + contract(db, wu_refs[q][...], 1, 1)
-        pg = jnp.sum(h * dh, axis=1, keepdims=True)
+        pg = h * dh
         part_x = px if part_x is None else part_x + px
         part_g = pg if part_g is None else part_g + pg
-    n_rows = n_own * capacity
-    for p in range(n_msgs // n_own):
-        rows = slice(p * n_rows, (p + 1) * n_rows)
-        back[p][:, 0:width] = part_x[rows, :].astype(BF16)
-        back[p][:, width:] = jnp.broadcast_to(part_g[rows, :], (n_rows, LANES)).astype(BF16)
-
-
-def weight_kernel(counts, capacity, quarter, has_received, *refs):
+    high = part_g.astype(BF16)
+    low = (part_g - high.astype(F32)).astype(BF16)
+    ones = jnp.ones((SUBLANES, part_g.shape[1]), BF16)
+    m = 0
+    for target in [back[p * len(chunks) + c] for p in range(n_parts) for c in range(len(chunks))]:
+        count = target.shape[0] // (part_x.shape[1] // LANES * capacity + SUBLANES)
+        for i in range(count):
+            rows = slice(m * capacity, (m + 1) * capacity)
+            sums = contract(ones, high[rows, :], 1, 1) + contract(ones, low[rows, :], 1, 1)
+            pack(target, i, capacity, part_x[rows, :], sums)
+            m += 1
+
+
+def weight_kernel(counts, capacity, quarter, *refs):
     n_msgs = sum(counts)
     msgs, refs = refs[:n_msgs], refs[n_msgs:]
     das, refs = refs[: len(counts)], refs[len(counts) :]
     dbs, refs = refs[: len(counts)], refs[len(counts) :]
-    hs, refs = refs[: len(counts)], refs[len(counts) :]
-    received, outs = (refs[:3], refs[3:]) if has_received else (None, refs)
+    hs, outs = refs[: len(counts)], refs[len(counts) :]
     hidden = outs[2].shape[0]
     cols = slice(quarter * hidden, (quarter + 1) * hidden)
     x = jnp.concatenate([m[0:capacity, :] for m in msgs], axis=0)
@@ -89,52 +129,65 @@
     da = jnp.concatenate([r[:, cols] for r in das], axis=0)
     db = jnp.concatenate([r[:, cols] for r in dbs], axis=0)
     h = jnp.concatenate([r[:, cols] for r in hs], axis=0)
-    results = (contract(x, da, 0, 0), contract(x, db, 0, 0), contract(h, gw, 0, 0))
-    for i in range(3):
-        total = results[i]
-        if has_received:
-            total = total + received[i][...].astype(F32)
-        outs[i][...] = total.astype(BF16)
-
-
-def sum_kernel(n_parts, capacity, *refs):
+    for out, total in zip(outs, (contract(x, da, 0, 0), contract(x, db, 0, 0), contract(h, gw, 0, 0))):
+        out[...] = total.astype(out.dtype)
+
+
+def add_kernel(*refs):
+    for own, received, out in zip(refs[:3], refs[3:6], refs[6:]):
+        out[...] = (own[...] + received[...].astype(F32)).astype(BF16)
+
+
+def sum_kernel(n_parts, *refs):
+    outs = refs[n_parts:]
     total = refs[0][...].astype(F32)
-    for p in range(1, n_parts):
-        total = total + refs[p][...].astype(F32)
-    for m, out in enumerate(refs[n_parts:]):
-        out[...] = total[m * capacity : (m + 1) * capacity, :].astype(BF16)
-
-
-def combine_kernel(n_experts, capacity, me_ref, exp_ref, keep_ref, gate_ref, table_ref, *refs):
+    for part in refs[1:n_parts]:
+        total = total + part[...].astype(F32)
+    rows = total.shape[0] // len(outs)
+    for i, out in enumerate(outs):
+        out[...] = total[i * rows : (i + 1) * rows, :].astype(BF16)
+
+
+def combine_kernel(n_experts, capacity, me_ref, exp_ref, ratio_ref, table_ref, *refs):
     msgs, (dtok_ref, dgate_ref) = refs[:n_experts], refs[n_experts:]
-    width = dtok_ref.shape[1]
-    rows = jnp.concatenate([m[:, 0:width] for m in msgs], axis=0)
-    dtok_ref[...] = contract(table_ref[...], rows, 0, 0).astype(BF16)
+    blocks = dtok_ref.shape[1] // LANES
+    rows = []
+    for m in msgs:
+        rows.append(jnp.concatenate([m[j * capacity : (j + 1) * capacity, :] for j in range(blocks)], axis=1))
+    dtok_ref[...] = contract(table_ref[...], jnp.concatenate(rows, axis=0), 0, 0).astype(BF16)
     d_gates = jnp.zeros(exp_ref.shape, F32)
     for k in range(n_experts):
-        value = contract(msgs[k][:, width:], table_ref[k * capacity : (k + 1) * capacity, :], 0, 0)
+        sums = msgs[k][blocks * capacity :, 0:capacity]
+        value = contract(sums, table_ref[k * capacity : (k + 1) * capacity, :], 1, 0)
         d_gates = d_gates + jnp.where(exp_ref[...] == (me_ref[0] ^ k), value[0 : exp_ref.shape[0], :], 0.0)
-    d_gates = d_gates * keep_ref[...].astype(F32) / gate_ref[...].astype(F32)
-    dgate_ref[...] = d_gates.astype(BF16)
-
-
-def call(body, outs, n_in, smem=0, cost=None):
-    vmem = pl.BlockSpec(memory_space=pltpu.VMEM)
-    scalar = pl.BlockSpec(memory_space=pltpu.SMEM)
+    dgate_ref[...] = (d_gates * ratio_ref[...]).astype(BF16)
+
+
+def call(body, outs, n_in, smem=0, hbm=0, scratch=()):
+    def spec(space):
+        return pl.BlockSpec(memory_space=space)
+
+    outs = [out if isinstance(out, jax.ShapeDtypeStruct) else jax.ShapeDtypeStruct(out, BF16) for out in outs]
     return pl.pallas_call(
         body,
-        out_shape=[jax.ShapeDtypeStruct(shape, BF16) for shape in outs],
-        in_specs=[scalar] * smem + [vmem] * (n_in - smem),
-        out_specs=[vmem] * len(outs),
-        cost_estimate=cost,
+        out_shape=outs,
+        in_specs=[spec(pltpu.SMEM)] * smem
+        + [spec(pltpu.HBM)] * hbm
+        + [spec(pltpu.VMEM)] * (n_in - smem - hbm),
+        out_specs=[spec(pltpu.VMEM)] * len(outs),
+        scratch_shapes=list(scratch),
         compiler_params=pltpu.CompilerParams(vmem_limit_bytes=VMEM_LIMIT),
     )
 
 
+def chunks_of(n_experts):
+    size = n_experts // 4
+    return [list(range(i * size, (i + 1) * size)) for i in range(4)]
+
+
 def groups_of(n_experts):
-    half = n_experts // 2
-    groups = ([0, 1, half], [k for k in range(2, half)] + [half + 1], list(range(half + 2, n_experts)))
-    return {f"g{i}": g for i, g in enumerate(groups) if g}
+    first, second, third, fourth = chunks_of(n_experts)
+    return [[first, second], [third], [fourth]]
 
 
 def local_tiled(tokens, cotangent, gates, experts, keep, gate_w, up_w, down_w):
@@ -148,50 +201,75 @@
     hidden = gate_w.shape[2]
     capacity = 3 * tok_rows // n_experts
     me = lax.axis_index("ep").astype(jnp.int32).reshape(1)
-    route = (me, experts.T, keep.T, gates.T)
+    route = (experts.T, keep.T, gates.T)
 
     def exchange(value, axis, size, bit):
         return lax.ppermute(value, axis, [(i, i ^ bit) for i in range(size)])
 
-    def run(body, outs, *args, smem=0):
-        return call(body, outs, len(args), smem=smem)(*args)
-
-    weights = []
-    for w in (gate_w, up_w, down_w):
-        weights += [w[0], exchange(w[0], "zr", n_groups, 1)]
-
-    outs = [(n_experts * capacity, tok_rows)] + [(2 * capacity, width)] * n_experts
-    table, *sends = run(functools.partial(send_kernel, n_experts, capacity), outs, *route, tokens, cotangent, smem=1)
+    def run(body, outs, *args, **kinds):
+        return call(body, outs, len(args), **kinds)(*args)
+
+    held = [pltpu.with_memory_space_constraint(w[0], pltpu.HBM) for w in (gate_w, up_w, down_w)]
+    swapped = [exchange(w[0], "zr", n_groups, 1) for w in (gate_w, up_w, down_w)]
+    sems = pltpu.SemaphoreType.DMA
+    held = run(stage_kernel, [w.shape for w in held], *held, hbm=3, scratch=[sems((3,))])
+    weights = [w for pair in zip(held, swapped) for w in pair]
+
+    inputs = [pltpu.with_memory_space_constraint(v, pltpu.HBM) for v in (*route, tokens, cotangent)]
+    outs = [(n_experts * capacity, tok_rows), jax.ShapeDtypeStruct(route[0].shape, jnp.int32)]
+    outs += [jax.ShapeDtypeStruct(route[0].shape, F32)] + [(2 * capacity, width)] * n_experts
+    table, named, ratio, *sends = run(
+        functools.partial(send_kernel, n_experts, capacity),
+        outs,
+        me,
+        *inputs,
+        smem=1,
+        hbm=len(inputs),
+        scratch=[pltpu.VMEM(v.shape, v.dtype) for v in inputs] + [sems((len(inputs),))],
+    )
     mine = [exchange(sends[k], "ep", n_experts, k) if k else sends[0] for k in range(n_experts)]
     peers = list(range(2, n_groups, 2))
     theirs = [[exchange(mine[k], "zr", n_groups, r) for r in peers] for k in range(n_experts)]
 
+    n_parts = 1 + len(peers)
+    msg_rows = width // LANES * capacity + SUBLANES
     all_msgs, counts, das, dbs, hs, returned = [], [], [], [], [], {}
-    for group in groups_of(n_experts).values():
+    for chunks in groups_of(n_experts):
+        group = sum(chunks, [])
         msgs = [mine[k] for k in group] + [theirs[k][p] for p in range(len(peers)) for k in group]
-        n_rows, n_own = len(msgs) * capacity, len(group) * capacity
-        outs = [(n_own, width + LANES)] * (1 + len(peers)) + [(n_rows, 2 * hidden)] * 3
-        body = functools.partial(grad_kernel, len(msgs), len(group), capacity)
+        outs = [(len(chunk) * msg_rows, LANES) for chunk in chunks] * n_parts
+        outs += [(len(msgs) * capacity, 2 * hidden)] * 3
+        body = functools.partial(grad_kernel, n_parts, [len(chunk) for chunk in chunks], capacity)
         *back, da, db, h = run(body, outs, *msgs, *weights)
         all_msgs, counts = all_msgs + msgs, counts + [len(msgs)]
         das, dbs, hs = das + [da], dbs + [db], hs + [h]
-        parts = [back[0]] + [exchange(back[1 + p], "zr", n_groups, r) for p, r in enumerate(peers)]
-        body = functools.partial(sum_kernel, len(parts), capacity)
-        summed = run(body, [(capacity, width + LANES)] * len(group), *parts)
-        for i, k in enumerate(group):
-            returned[k] = exchange(summed[i], "ep", n_experts, k) if k else summed[i]
-
-    w_outs = [(width, hidden), (width, hidden), (hidden, width)]
+        for c, chunk in enumerate(chunks):
+            parts = [back[c]]
+            for p, r in enumerate(peers):
+                parts.append(exchange(back[(p + 1) * len(chunks) + c], "zr", n_groups, r))
+            body = functools.partial(sum_kernel, n_parts)
+            summed = run(body, [(msg_rows, LANES)] * len(chunk), *parts)
+            for k, value in zip(chunk, summed):
+                returned[k] = exchange(value, "ep", n_experts, k) if k else value
+
+    shapes = [(width, hidden), (width, hidden), (hidden, width)]
     w_args = all_msgs + das + dbs + hs
-    partner = run(functools.partial(weight_kernel, counts, capacity, 1, False), w_outs, *w_args)
-    w_args = w_args + [exchange(w, "zr", n_groups, 1) for w in partner]
-    dwg, dwu, dwd = run(functools.partial(weight_kernel, counts, capacity, 0, True), w_outs, *w_args)
+    partner = run(functools.partial(weight_kernel, counts, capacity, 1), shapes, *w_args)
+    received = [exchange(w, "zr", n_groups, 1) for w in partner]
+    own = run(
+        functools.partial(weight_kernel, counts, capacity, 0),
+        [jax.ShapeDtypeStruct(shape, F32) for shape in shapes],
+        *w_args,
+    )
+    dwg, dwu, dwd = run(add_kernel, shapes, *own, *received)
 
     outs = [(tok_rows, width), experts.T.shape]
     d_tokens, d_gates = run(
         functools.partial(combine_kernel, n_experts, capacity),
         outs,
-        *route,
+        me,
+        named,
+        ratio,
         table,
         *[returned[k] for k in range(n_experts)],
         smem=1,

time: 125 us -> 110 us (0.88)
  starting transfers between devices: 50.1 us -> 41.3 us
  local copies, waits for them, and re-layouts: 6.74 us -> 0.01 us
  Pallas kernels: 13.1 us -> 16.1 us
  waiting for transfers between devices: 54 us -> 51.9 us
    ppermute x31 -> x32, starting transfers between devices: 50.1 us -> 41.3 us  [exchange(): return lax.ppermute(value, axis, [(i, i ^ bit) for i in range(size)])]
    unnamed x26 -> x2, local copies, waits for them, and re-layouts: 6.74 us -> 0.01 us
    pallas_call x10 -> x13, Pallas kernels: 13.1 us -> 16.1 us  [run(): return call(body, outs, len(args), **kinds)(*args)]
    ppermute x31 -> x32, waiting for transfers between devices: 54 us -> 51.9 us  [exchange(): return lax.ppermute(value, axis, [(i, i ^ bit) for i in range(size)])]
  transfers between devices with their start and end apart: 31 -> 32, of which waited for: 16 -> 16; matrix products, arithmetic and copies ran while one was open for 0% -> 0% of each run, Pallas kernels for 8% -> 12%
where the time goes in v1:
time: 110 us
  waiting for transfers between devices  51.9 us (47%)
  starting transfers between devices  41.3 us (38%)
  Pallas kernels  16.1 us (15%)
    ppermute x32, waiting for transfers between devices, exchange(): return lax.ppermute(value, axis, [(i, i ^ bit) for i in range(size)])  51.9 us
    ppermute x32, starting transfers between devices, exchange(): return lax.ppermute(value, axis, [(i, i ^ bit) for i in range(size)])  41.3 us
    pallas_call x13, Pallas kernels, run(): return call(body, outs, len(args), **kinds)(*args)  16.1 us
  transfers between devices with their start and end apart: 32, of which 16 were waited for; matrix products, arithmetic and copies ran while one was open for 0% of the time, Pallas kernels for 12%

profile of v1, /device:TPU:0, one launch (start us, length us, event | category | flops | bytes accessed | tf_op | source)
XLA Modules:
  0.0 110.1 jit_solution(5622991778062873546)
XLA Ops:
  0.6 0.0 copy-start
  0.6 1.9 %shard_map.119 = (bf16[384,128]{1,0:T(8,128)(2,1)S(1)}, s32[2,128]{1,0:T(2,128)S(1)}, f32[2,128]{1,0:T(2,128)S(1)}, bf16[96,1024]{1,0:T(8,128)(2,1)S(1)}, bf16[9...) custom-call(s32[1]{0:T(128)} %bitcast.me_ref, ...), custom_call_target="tpu_custom_call" | custom-call | tf_op jit(solution)/shard_map/pallas_call | solution.py:210
  2.5 3.1 %collective-permute-start = (bf16[96,1024]{1,0:T(8,128)(2,1)S(1)}, bf16[96,1024]{1,0:T(8,128)(2,1)S(1)}, u32[]{:S(2)}, u32[]{:S(2)}) collective-permute-start(bf16[96,1024]{1,0:T(8,128)(2,1)S(1)} %get-tuple-element.59), channel_id=1, source_target_pairs={{0,4},{4,0},{8,12},{12,8},{16,20},{20,16},{24,28},{28,24},{1,5},{5... | collective-permute-start | bytes 589832 | tf_op jit(solution)/shard_map/ppermute | solution.py:207
  5.6 1.6 %collective-permute-start.1 = (bf16[96,1024]{1,0:T(8,128)(2,1)S(1)}, bf16[96,1024]{1,0:T(8,128)(2,1)S(1)}, u32[]{:S(2)}, u32[]{:S(2)}) collective-permute-start(bf16[96,1024]{1,0:T(8,128)(2,1)S(1)} %get-tuple-element.60), channel_id=1, source_target_pairs={{0,8},{4,12},{8,0},{12,4},{16,24},{20,28},{24,16},{28,20},{1,9},{5... | collective-permute-start | bytes 589832 | tf_op jit(solution)/shard_map/ppermute | solution.py:207
  7.2 0.0 collective-permute-start.2
  7.2 1.9 %collective-permute-start.3 = (bf16[96,1024]{1,0:T(8,128)(2,1)S(1)}, bf16[96,1024]{1,0:T(8,128)(2,1)S(1)}, u32[]{:S(2)}, u32[]{:S(2)}) collective-permute-start(bf16[96,1024]{1,0:T(8,128)(2,1)S(1)} %get-tuple-element.58.refs_0_), channel_id=1, source_target_pairs={{0,2},{1,3},{2,0},{3,1},{4,6},{5,7},{6,4},{7,5},{8,10},{9,11},{10,... | collective-permute-start | bytes 589832 | tf_op jit(solution)/shard_map/ppermute | solution.py:207
  9.1 2.6 %collective-permute-start.15 = (bf16[96,1024]{1,0:T(8,128)(2,1)S(1)}, bf16[96,1024]{1,0:T(8,128)(2,1)S(1)}, u32[]{:S(2)}, u32[]{:S(2)}) collective-permute-start(bf16[96,1024]{1,0:T(8,128)(2,1)S(1)} %get-tuple-element.73), channel_id=1, source_target_pairs={{0,16},{4,20},{8,24},{12,28},{16,0},{20,4},{24,8},{28,12},{1,17},{... | collective-permute-start | bytes 589832 | tf_op jit(solution)/shard_map/ppermute | solution.py:207
  11.7 0.0 collective-permute-start.7
  11.7 5.9 %collective-permute-done.1.refs_2_ = bf16[96,1024]{1,0:T(8,128)(2,1)S(1)} collective-permute-done((bf16[96,1024]{1,0:T(8,128)(2,1)S(1)}, bf16[96,1024]{1,0:T(8,128)(2,1)S(1)}, u32[]{:S(2)}, u32[]{:S(2)}) %collective-permute-start.1) | collective-permute-done | bytes 196640 | tf_op jit(solution)/shard_map/ppermute | solution.py:207
  17.6 0.0 collective-permute-start.8
  17.6 2.6 %collective-permute-done.2.refs_3_ = bf16[96,1024]{1,0:T(8,128)(2,1)S(1)} collective-permute-done((bf16[96,1024]{1,0:T(8,128)(2,1)S(1)}, bf16[96,1024]{1,0:T(8,128)(2,1)S(1)}, u32[]{:S(2)}, u32[]{:S(2)}) %collective-permute-start.2) | collective-permute-done | bytes 196640 | tf_op jit(solution)/shard_map/ppermute | solution.py:207
  20.2 1.2 %collective-permute-start.16 = (bf16[96,1024]{1,0:T(8,128)(2,1)S(1)}, bf16[96,1024]{1,0:T(8,128)(2,1)S(1)}, u32[]{:S(2)}, u32[]{:S(2)}) collective-permute-start(bf16[96,1024]{1,0:T(8,128)(2,1)S(1)} %get-tuple-element.74), channel_id=1, source_target_pairs={{0,20},{4,16},{8,28},{12,24},{16,4},{20,0},{24,12},{28,8},{1,21},{... | collective-permute-start | bytes 589832 | tf_op jit(solution)/shard_map/ppermute | solution.py:207
  21.4 0.0 collective-permute-done.3.refs_4_
  21.4 2.1 %collective-permute-start.4 = (bf16[96,1024]{1,0:T(8,128)(2,1)S(1)}, bf16[96,1024]{1,0:T(8,128)(2,1)S(1)}, u32[]{:S(2)}, u32[]{:S(2)}) collective-permute-start(bf16[96,1024]{1,0:T(8,128)(2,1)S(1)} %collective-permute-done.refs_1_), channel_id=1, source_target_pairs={{0,2},{1,3},{2,0},{3,1},{4,6},{5,7},{6,4},{7,5},{8,10},{9,11},{10,... | collective-permute-start | bytes 589832 | tf_op jit(solution)/shard_map/ppermute | solution.py:207
  23.5 0.0 collective-permute-start.9
  23.5 8.5 %collective-permute-done.16.refs_1_.refs_9_ = bf16[96,1024]{1,0:T(8,128)(2,1)S(1)} collective-permute-done((bf16[96,1024]{1,0:T(8,128)(2,1)S(1)}, bf16[96,1024]{1,0:T(8,128)(2,1)S(1)}, u32[]{:S(2)}, u32[]{:S(2)}) %collective-permute-start.16) | collective-permute-done | bytes 196640 | tf_op jit(solution)/shard_map/ppermute | solution.py:207
  32.0 1.4 %collective-permute-start.5 = (bf16[96,1024]{1,0:T(8,128)(2,1)S(1)}, bf16[96,1024]{1,0:T(8,128)(2,1)S(1)}, u32[]{:S(2)}, u32[]{:S(2)}) collective-permute-start(bf16[96,1024]{1,0:T(8,128)(2,1)S(1)} %collective-permute-done.1.refs_2_), channel_id=1, source_target_pairs={{0,2},{1,3},{2,0},{3,1},{4,6},{5,7},{6,4},{7,5},{8,10},{9,11},{10,... | collective-permute-start | bytes 589832 | tf_op jit(solution)/shard_map/ppermute | solution.py:207
  33.4 0.7 collective-permute-start.6
  34.0 5.7 %collective-permute-done.5.refs_6_ = bf16[96,1024]{1,0:T(8,128)(2,1)S(1)} collective-permute-done((bf16[96,1024]{1,0:T(8,128)(2,1)S(1)}, bf16[96,1024]{1,0:T(8,128)(2,1)S(1)}, u32[]{:S(2)}, u32[]{:S(2)}) %collective-permute-start.5) | collective-permute-done | bytes 196640 | tf_op jit(solution)/shard_map/ppermute | solution.py:207
  39.8 2.5 %collective-permute-start.22 = (bf16[96,1024]{1,0:T(8,128)(2,1)S(1)}, bf16[96,1024]{1,0:T(8,128)(2,1)S(1)}, u32[]{:S(2)}, u32[]{:S(2)}) collective-permute-start(bf16[96,1024]{1,0:T(8,128)(2,1)S(1)} %get-tuple-element.79), channel_id=1, source_target_pairs={{0,24},{4,28},{8,16},{12,20},{16,8},{20,12},{24,0},{28,4},{1,25},{... | collective-permute-start | bytes 589832 | tf_op jit(solution)/shard_map/ppermute | solution.py:207
  42.3 2.9 %collective-permute-start.23 = (bf16[96,1024]{1,0:T(8,128)(2,1)S(1)}, bf16[96,1024]{1,0:T(8,128)(2,1)S(1)}, u32[]{:S(2)}, u32[]{:S(2)}) collective-permute-start(bf16[96,1024]{1,0:T(8,128)(2,1)S(1)} %get-tuple-element.80), channel_id=1, source_target_pairs={{0,28},{4,24},{8,20},{12,16},{16,12},{20,8},{24,4},{28,0},{1,29},{... | collective-permute-start | bytes 589832 | tf_op jit(solution)/shard_map/ppermute | solution.py:207
  45.2 0.0 collective-permute-done.7.refs_9_.refs_5_
  45.2 1.7 %collective-permute-start.17 = (bf16[96,1024]{1,0:T(8,128)(2,1)S(1)}, bf16[96,1024]{1,0:T(8,128)(2,1)S(1)}, u32[]{:S(2)}, u32[]{:S(2)}) collective-permute-start(bf16[96,1024]{1,0:T(8,128)(2,1)S(1)} %collective-permute-done.15.refs_0_.refs_8_), channel_id=1, source_target_pairs={{0,2},{1,3},{2,0},{3,1},{4,6},{5,7},{6,4},{7,5},{8,10},{9,11},{10,... | collective-permute-start | bytes 589832 | tf_op jit(solution)/shard_map/ppermute | solution.py:207
  46.9 0.0 collective-permute-done.8.refs_11_.refs_7_
  46.9 0.3 collective-permute-start.18
  47.2 1.4 %shard_map.120 = (bf16[1024,256]{1,0:T(8,128)(2,1)S(1)}, bf16[1024,256]{1,0:T(8,128)(2,1)S(1)}, bf16[256,1024]{1,0:T(8,128)(2,1)S(1)}) custom-call(bf16[1024,256]{1,0:T(8,128)(2,1)} %bitcast.11, bf16[1024,256]{1,0:T(8,128)(2,1)} %bitcast.14, bf16[256,1024]{1,0:T(8,128)(2,1)} %bitcast.16), custom_call_target="tpu_custom_call" | custom-call | tf_op jit(solution)/shard_map/pallas_call | solution.py:210
  48.6 0.0 collective-permute-done.9.refs_13_.refs_9_
  48.6 3.5 %shard_map.121 = (bf16[784,128]{1,0:T(8,128)(2,1)S(1)}, bf16[784,128]{1,0:T(8,128)(2,1)S(1)}, bf16[784,128]{1,0:T(8,128)(2,1)S(1)}, bf16[784,128]{1,0:T(8,128)(2...) custom-call(bf16[96,1024]{1,0:T(8,128)(2,1)S(1)} %get-tuple-element.58.refs_0_, ...), custom_call_target="tpu_custom_call" | custom-call | tf_op jit(solution)/shard_map/pallas_call | solution.py:210
  52.1 1.8 %collective-permute-start.10 = (bf16[784,128]{1,0:T(8,128)(2,1)S(1)}, bf16[784,128]{1,0:T(8,128)(2,1)S(1)}, u32[]{:S(2)}, u32[]{:S(2)}) collective-permute-start(bf16[784,128]{1,0:T(8,128)(2,1)S(1)} %get-tuple-element.66), channel_id=1, source_target_pairs={{0,2},{1,3},{2,0},{3,1},{4,6},{5,7},{6,4},{7,5},{8,10},{9,11},{10,... | collective-permute-start | bytes 602120 | tf_op jit(solution)/shard_map/ppermute | solution.py:207
  53.9 0.0 collective-permute-done.22.refs_0_.refs_12_
  53.9 0.3 collective-permute-start.24
  54.2 0.0 collective-permute-done.23.refs_1_.refs_13_
  54.2 1.7 %collective-permute-start.25 = (bf16[96,1024]{1,0:T(8,128)(2,1)S(1)}, bf16[96,1024]{1,0:T(8,128)(2,1)S(1)}, u32[]{:S(2)}, u32[]{:S(2)}) collective-permute-start(bf16[96,1024]{1,0:T(8,128)(2,1)S(1)} %collective-permute-done.23.refs_1_.refs_13_), channel_id=1, source_target_pairs={{0,2},{1,3},{2,0},{3,1},{4,6},{5,7},{6,4},{7,5},{8,10},{9,11},{10,... | collective-permute-start | bytes 589832 | tf_op jit(solution)/shard_map/ppermute | solution.py:207
  55.9 0.3 collective-permute-start.12
  56.2 0.9 collective-permute-done.18.refs_3_.refs_11_
  57.1 2.0 %shard_map.124 = (bf16[784,128]{1,0:T(8,128)(2,1)S(1)}, bf16[784,128]{1,0:T(8,128)(2,1)S(1)}, bf16[192,512]{1,0:T(8,128)(2,1)S(1)}, bf16[192,512]{1,0:T(8,128)(2,1)S(1)}, bf16[192,512]{1,0:T(8,128)(2,1)S(1)}) custom-call(bf16[96,1024]{1,0:T(8,128)(2,1)S(1)} %collective-permute-done.15.refs_0_.refs_8_, ...), custom_call_target="tpu_custom_call" | custom-call | tf_op jit(solution)/shard_map/pallas_call | solution.py:210
  59.1 1.7 %collective-permute-start.19 = (bf16[784,128]{1,0:T(8,128)(2,1)S(1)}, bf16[784,128]{1,0:T(8,128)(2,1)S(1)}, u32[]{:S(2)}, u32[]{:S(2)}) collective-permute-start(bf16[784,128]{1,0:T(8,128)(2,1)S(1)} %get-tuple-element.76), channel_id=1, source_target_pairs={{0,2},{1,3},{2,0},{3,1},{4,6},{5,7},{6,4},{7,5},{8,10},{9,11},{10,... | collective-permute-start | bytes 602120 | tf_op jit(solution)/shard_map/ppermute | solution.py:207
  60.8 4.9 %collective-permute-done.24.refs_2_.refs_14_ = bf16[96,1024]{1,0:T(8,128)(2,1)S(1)} collective-permute-done((bf16[96,1024]{1,0:T(8,128)(2,1)S(1)}, bf16[96,1024]{1,0:T(8,128)(2,1)S(1)}, u32[]{:S(2)}, u32[]{:S(2)}) %collective-permute-start.24) | collective-permute-done | bytes 196640 | tf_op jit(solution)/shard_map/ppermute | solution.py:207
  65.7 4.2 %collective-permute-done.25.refs_3_.refs_15_ = bf16[96,1024]{1,0:T(8,128)(2,1)S(1)} collective-permute-done((bf16[96,1024]{1,0:T(8,128)(2,1)S(1)}, bf16[96,1024]{1,0:T(8,128)(2,1)S(1)}, u32[]{:S(2)}, u32[]{:S(2)}) %collective-permute-start.25) | collective-permute-done | bytes 196640 | tf_op jit(solution)/shard_map/ppermute | solution.py:207
  69.9 2.0 %shard_map.126 = (bf16[784,128]{1,0:T(8,128)(2,1)S(1)}, bf16[784,128]{1,0:T(8,128)(2,1)S(1)}, bf16[192,512]{1,0:T(8,128)(2,1)S(1)}, bf16[192,512]{1,0:T(8,128)(2,1)S(1)}, bf16[192,512]{1,0:T(8,128)(2,1)S(1)}) custom-call(bf16[96,1024]{1,0:T(8,128)(2,1)S(1)} %collective-permute-done.22.refs_0_.refs_12_, ...), custom_call_target="tpu_custom_call" | custom-call | tf_op jit(solution)/shard_map/pallas_call | solution.py:210
  71.8 1.4 %shard_map.130 = (bf16[1024,256]{1,0:T(8,128)(2,1)S(1)}, bf16[1024,256]{1,0:T(8,128)(2,1)S(1)}, bf16[256,1024]{1,0:T(8,128)(2,1)S(1)}) custom-call(bf16[96,1024]{1,0:T(8,128)(2,1)S(1)} %get-tuple-element.58.refs_0_, bf16[96,1024]{1,0:T(8,128)(2,1)S(1)} %collective-permute-done.refs_1_, bf16[96,1024]{1,0:T(8,128)(2,1)S(1)} %collective-permute-done.1.refs_2_, ...), custom_call_target="tpu_custom_call" | custom-call | tf_op jit(solution)/shard_map/pallas_call | solution.py:210
  73.3 0.1 collective-permute-start.29
  73.4 0.5 collective-permute-start.30
  73.9 0.1 collective-permute-start.31
  73.9 0.2 collective-permute-done.12.refs_1_
  74.2 1.6 %collective-permute-start.26 = (bf16[784,128]{1,0:T(8,128)(2,1)S(1)}, bf16[784,128]{1,0:T(8,128)(2,1)S(1)}, u32[]{:S(2)}, u32[]{:S(2)}) collective-permute-start(bf16[784,128]{1,0:T(8,128)(2,1)S(1)} %get-tuple-element.82), channel_id=1, source_target_pairs={{0,2},{1,3},{2,0},{3,1},{4,6},{5,7},{6,4},{7,5},{8,10},{9,11},{10,... | collective-permute-start | bytes 602120 | tf_op jit(solution)/shard_map/ppermute | solution.py:207
  75.8 0.7 collective-permute-done.19.refs_1_
  76.5 1.6 %collective-permute-start.11 = (bf16[392,128]{1,0:T(8,128)(2,1)S(1)}, bf16[392,128]{1,0:T(8,128)(2,1)S(1)}, u32[]{:S(2)}, u32[]{:S(2)}) collective-permute-start(bf16[392,128]{1,0:T(8,128)(2,1)S(1)} %get-tuple-element.68), channel_id=1, source_target_pairs={{0,4},{4,0},{8,12},{12,8},{16,20},{20,16},{24,28},{28,24},{1,5},{5... | collective-permute-start | bytes 301064 | tf_op jit(solution)/shard_map/ppermute | solution.py:207
  78.2 3.1 %collective-permute-done.26.refs_1_ = bf16[784,128]{1,0:T(8,128)(2,1)S(1)} collective-permute-done((bf16[784,128]{1,0:T(8,128)(2,1)S(1)}, bf16[784,128]{1,0:T(8,128)(2,1)S(1)}, u32[]{:S(2)}, u32[]{:S(2)}) %collective-permute-start.26) | collective-permute-done | bytes 200736 | tf_op jit(solution)/shard_map/ppermute | solution.py:207
  81.3 0.0 collective-permute-start.13
  81.3 3.1 %collective-permute-start.14 = (bf16[392,128]{1,0:T(8,128)(2,1)S(1)}, bf16[392,128]{1,0:T(8,128)(2,1)S(1)}, u32[]{:S(2)}, u32[]{:S(2)}) collective-permute-start(bf16[392,128]{1,0:T(8,128)(2,1)S(1)} %get-tuple-element.72), channel_id=1, source_target_pairs={{0,12},{4,8},{8,4},{12,0},{16,28},{20,24},{24,20},{28,16},{1,13},{... | collective-permute-start | bytes 301064 | tf_op jit(solution)/shard_map/ppermute | solution.py:207
  84.4 2.0 %collective-permute-done.13.refs_2_ = bf16[392,128]{1,0:T(8,128)(2,1)S(1)} collective-permute-done((bf16[392,128]{1,0:T(8,128)(2,1)S(1)}, bf16[392,128]{1,0:T(8,128)(2,1)S(1)}, u32[]{:S(2)}, u32[]{:S(2)}) %collective-permute-start.13) | collective-permute-done | bytes 100384 | tf_op jit(solution)/shard_map/ppermute | solution.py:207
  86.4 1.1 collective-permute-start.20
  87.5 1.1 collective-permute-done.14.refs_3_
  88.6 1.9 %collective-permute-start.21 = (bf16[392,128]{1,0:T(8,128)(2,1)S(1)}, bf16[392,128]{1,0:T(8,128)(2,1)S(1)}, u32[]{:S(2)}, u32[]{:S(2)}) collective-permute-start(bf16[392,128]{1,0:T(8,128)(2,1)S(1)} %get-tuple-element.78), channel_id=1, source_target_pairs={{0,20},{4,16},{8,28},{12,24},{16,4},{20,0},{24,12},{28,8},{1,21},{... | collective-permute-start | bytes 301064 | tf_op jit(solution)/shard_map/ppermute | solution.py:207
  90.5 6.3 %collective-permute-done.20.refs_4_ = bf16[392,128]{1,0:T(8,128)(2,1)S(1)} collective-permute-done((bf16[392,128]{1,0:T(8,128)(2,1)S(1)}, bf16[392,128]{1,0:T(8,128)(2,1)S(1)}, u32[]{:S(2)}, u32[]{:S(2)}) %collective-permute-start.20) | collective-permute-done | bytes 100384 | tf_op jit(solution)/shard_map/ppermute | solution.py:207
  96.8 2.1 %collective-permute-start.27 = (bf16[392,128]{1,0:T(8,128)(2,1)S(1)}, bf16[392,128]{1,0:T(8,128)(2,1)S(1)}, u32[]{:S(2)}, u32[]{:S(2)}) collective-permute-start(bf16[392,128]{1,0:T(8,128)(2,1)S(1)} %get-tuple-element.83), channel_id=1, source_target_pairs={{0,24},{4,28},{8,16},{12,20},{16,8},{20,12},{24,0},{28,4},{1,25},{... | collective-permute-start | bytes 301064 | tf_op jit(solution)/shard_map/ppermute | solution.py:207
  98.9 1.4 %collective-permute-done.21.refs_5_ = bf16[392,128]{1,0:T(8,128)(2,1)S(1)} collective-permute-done((bf16[392,128]{1,0:T(8,128)(2,1)S(1)}, bf16[392,128]{1,0:T(8,128)(2,1)S(1)}, u32[]{:S(2)}, u32[]{:S(2)}) %collective-permute-start.21) | collective-permute-done | bytes 100384 | tf_op jit(solution)/shard_map/ppermute | solution.py:207
  100.3 1.7 %collective-permute-start.28 = (bf16[392,128]{1,0:T(8,128)(2,1)S(1)}, bf16[392,128]{1,0:T(8,128)(2,1)S(1)}, u32[]{:S(2)}, u32[]{:S(2)}) collective-permute-start(bf16[392,128]{1,0:T(8,128)(2,1)S(1)} %get-tuple-element.84), channel_id=1, source_target_pairs={{0,28},{4,24},{8,20},{12,16},{16,12},{20,8},{24,4},{28,0},{1,29},{... | collective-permute-start | bytes 301064 | tf_op jit(solution)/shard_map/ppermute | solution.py:207
  102.0 1.4 %shard_map.129 = (f32[1024,256]{1,0:T(8,128)S(1)}, f32[1024,256]{1,0:T(8,128)S(1)}, f32[256,1024]{1,0:T(8,128)S(1)}) custom-call(bf16[96,1024]{1,0:T(8,128)(2,1)S(1)} %get-tuple-element.58.refs_0_, bf16[96,1024]{1,0:T(8,128)(2,1)S(1)} %collective-permute-done.refs_1_, bf16[96,1024]{1,0:T(8,128)(2,1)S(1)} %collective-permute-done.1.refs_2_, ...), custom_call_target="tpu_custom_call" | custom-call | tf_op jit(solution)/shard_map/pallas_call | solution.py:210
  103.4 0.3 collective-permute-done.27.refs_6_
  103.7 4.0 %collective-permute-done.28.refs_7_ = bf16[392,128]{1,0:T(8,128)(2,1)S(1)} collective-permute-done((bf16[392,128]{1,0:T(8,128)(2,1)S(1)}, bf16[392,128]{1,0:T(8,128)(2,1)S(1)}, u32[]{:S(2)}, u32[]{:S(2)}) %collective-permute-start.28) | collective-permute-done | bytes 100384 | tf_op jit(solution)/shard_map/ppermute | solution.py:207
  107.7 1.0 shard_map.128
  108.7 1.4 %shard_map.131 = (bf16[1024,256]{1,0:T(8,128)(2,1)}, bf16[1024,256]{1,0:T(8,128)(2,1)}, bf16[256,1024]{1,0:T(8,128)(2,1)}) custom-call(f32[1024,256]{1,0:T(8,128)S(1)} %get-tuple-element.96.refs_0_, f32[1024,256]{1,0:T(8,128)S(1)} %get-tuple-element.97.refs_1_, f32[256,1024]{1,0:T(8,128)S(1)} %get-tuple-element.98.refs_2_, ...), custom_call_target="tpu_custom_call" | custom-call | tf_op jit(solution)/shard_map/pallas_call | solution.py:210
  (15 shorter events, 0.2 us)
Async XLA Ops:
  0.6 11.0 %copy-start = (bf16[1,1024,256]{2,1,0:T(8,128)(2,1)S(1)}, bf16[1,1024,256]{2,1,0:T(8,128)(2,1)}, u32[]{:S(2)}) copy-start(bf16[1,1024,256]{2,1,0:T(8,128)(2,1)} %param.13) | copy-start | bytes 1572868
  2.5 9.1 %collective-permute-start = (bf16[96,1024]{1,0:T(8,128)(2,1)S(1)}, bf16[96,1024]{1,0:T(8,128)(2,1)S(1)}, u32[]{:S(2)}, u32[]{:S(2)}) collective-permute-start(bf16[96,1024]{1,0:T(8,128)(2,1)S(1)} %get-tuple-element.59), channel_id=1, source_target_pairs={{0,4},{4,0},{8,12},{12,8},{16,20},{20,16},{24,28},{28,24},{1,5},{5... | collective-permute-start | bytes 589832 | tf_op jit(solution)/shard_map/ppermute | solution.py:207
  5.6 12.0 %collective-permute-start.1 = (bf16[96,1024]{1,0:T(8,128)(2,1)S(1)}, bf16[96,1024]{1,0:T(8,128)(2,1)S(1)}, u32[]{:S(2)}, u32[]{:S(2)}) collective-permute-start(bf16[96,1024]{1,0:T(8,128)(2,1)S(1)} %get-tuple-element.60), channel_id=1, source_target_pairs={{0,8},{4,12},{8,0},{12,4},{16,24},{20,28},{24,16},{28,20},{1,9},{5... | collective-permute-start | bytes 589832 | tf_op jit(solution)/shard_map/ppermute | solution.py:207
  7.2 13.0 %collective-permute-start.2 = (bf16[96,1024]{1,0:T(8,128)(2,1)S(1)}, bf16[96,1024]{1,0:T(8,128)(2,1)S(1)}, u32[]{:S(2)}, u32[]{:S(2)}) collective-permute-start(bf16[96,1024]{1,0:T(8,128)(2,1)S(1)} %get-tuple-element.61), channel_id=1, source_target_pairs={{0,12},{4,8},{8,4},{12,0},{16,28},{20,24},{24,20},{28,16},{1,13},{... | collective-permute-start | bytes 589832 | tf_op jit(solution)/shard_map/ppermute | solution.py:207
  7.2 14.2 %collective-permute-start.3 = (bf16[96,1024]{1,0:T(8,128)(2,1)S(1)}, bf16[96,1024]{1,0:T(8,128)(2,1)S(1)}, u32[]{:S(2)}, u32[]{:S(2)}) collective-permute-start(bf16[96,1024]{1,0:T(8,128)(2,1)S(1)} %get-tuple-element.58.refs_0_), channel_id=1, source_target_pairs={{0,2},{1,3},{2,0},{3,1},{4,6},{5,7},{6,4},{7,5},{8,10},{9,11},{10,... | collective-permute-start | bytes 589832 | tf_op jit(solution)/shard_map/ppermute | solution.py:207
  9.1 14.5 %collective-permute-start.15 = (bf16[96,1024]{1,0:T(8,128)(2,1)S(1)}, bf16[96,1024]{1,0:T(8,128)(2,1)S(1)}, u32[]{:S(2)}, u32[]{:S(2)}) collective-permute-start(bf16[96,1024]{1,0:T(8,128)(2,1)S(1)} %get-tuple-element.73), channel_id=1, source_target_pairs={{0,16},{4,20},{8,24},{12,28},{16,0},{20,4},{24,8},{28,12},{1,17},{... | collective-permute-start | bytes 589832 | tf_op jit(solution)/shard_map/ppermute | solution.py:207
  11.7 33.5 %collective-permute-start.7 = (bf16[1024,256]{1,0:T(8,128)(2,1)S(1)}, bf16[1024,256]{1,0:T(8,128)(2,1)S(1)}, u32[]{:S(2)}, u32[]{:S(2)}) collective-permute-start(bf16[1024,256]{1,0:T(8,128)(2,1)S(1)} %bitcast.12), channel_id=1, source_target_pairs={{0,1},{1,0},{2,3},{3,2},{4,5},{5,4},{6,7},{7,6},{8,9},{9,8},{10,11... | collective-permute-start | bytes 1572872 | tf_op jit(solution)/shard_map/ppermute | solution.py:207
  17.6 29.3 %collective-permute-start.8 = (bf16[1024,256]{1,0:T(8,128)(2,1)}, bf16[1024,256]{1,0:T(8,128)(2,1)S(1)}, u32[]{:S(2)}, u32[]{:S(2)}) collective-permute-start(bf16[1024,256]{1,0:T(8,128)(2,1)} %bitcast.13), channel_id=1, source_target_pairs={{0,1},{1,0},{2,3},{3,2},{4,5},{5,4},{6,7},{7,6},{8,9},{9,8},{10,11... | collective-permute-start | bytes 1572872 | tf_op jit(solution)/shard_map/ppermute | solution.py:207
  20.2 11.8 %collective-permute-start.16 = (bf16[96,1024]{1,0:T(8,128)(2,1)S(1)}, bf16[96,1024]{1,0:T(8,128)(2,1)S(1)}, u32[]{:S(2)}, u32[]{:S(2)}) collective-permute-start(bf16[96,1024]{1,0:T(8,128)(2,1)S(1)} %get-tuple-element.74), channel_id=1, source_target_pairs={{0,20},{4,16},{8,28},{12,24},{16,4},{20,0},{24,12},{28,8},{1,21},{... | collective-permute-start | bytes 589832 | tf_op jit(solution)/shard_map/ppermute | solution.py:207
  21.4 11.9 %collective-permute-start.4 = (bf16[96,1024]{1,0:T(8,128)(2,1)S(1)}, bf16[96,1024]{1,0:T(8,128)(2,1)S(1)}, u32[]{:S(2)}, u32[]{:S(2)}) collective-permute-start(bf16[96,1024]{1,0:T(8,128)(2,1)S(1)} %collective-permute-done.refs_1_), channel_id=1, source_target_pairs={{0,2},{1,3},{2,0},{3,1},{4,6},{5,7},{6,4},{7,5},{8,10},{9,11},{10,... | collective-permute-start | bytes 589832 | tf_op jit(solution)/shard_map/ppermute | solution.py:207
  23.5 25.1 %collective-permute-start.9 = (bf16[256,1024]{1,0:T(8,128)(2,1)}, bf16[256,1024]{1,0:T(8,128)(2,1)S(1)}, u32[]{:S(2)}, u32[]{:S(2)}) collective-permute-start(bf16[256,1024]{1,0:T(8,128)(2,1)} %bitcast.15), channel_id=1, source_target_pairs={{0,1},{1,0},{2,3},{3,2},{4,5},{5,4},{6,7},{7,6},{8,9},{9,8},{10,11... | collective-permute-start | bytes 1572872 | tf_op jit(solution)/shard_map/ppermute | solution.py:207
  32.0 7.8 %collective-permute-start.5 = (bf16[96,1024]{1,0:T(8,128)(2,1)S(1)}, bf16[96,1024]{1,0:T(8,128)(2,1)S(1)}, u32[]{:S(2)}, u32[]{:S(2)}) collective-permute-start(bf16[96,1024]{1,0:T(8,128)(2,1)S(1)} %collective-permute-done.1.refs_2_), channel_id=1, source_target_pairs={{0,2},{1,3},{2,0},{3,1},{4,6},{5,7},{6,4},{7,5},{8,10},{9,11},{10,... | collective-permute-start | bytes 589832 | tf_op jit(solution)/shard_map/ppermute | solution.py:207
  33.4 8.9 %collective-permute-start.6 = (bf16[96,1024]{1,0:T(8,128)(2,1)S(1)}, bf16[96,1024]{1,0:T(8,128)(2,1)S(1)}, u32[]{:S(2)}, u32[]{:S(2)}) collective-permute-start(bf16[96,1024]{1,0:T(8,128)(2,1)S(1)} %collective-permute-done.2.refs_3_), channel_id=1, source_target_pairs={{0,2},{1,3},{2,0},{3,1},{4,6},{5,7},{6,4},{7,5},{8,10},{9,11},{10,... | collective-permute-start | bytes 589832 | tf_op jit(solution)/shard_map/ppermute | solution.py:207
  39.8 14.1 %collective-permute-start.22 = (bf16[96,1024]{1,0:T(8,128)(2,1)S(1)}, bf16[96,1024]{1,0:T(8,128)(2,1)S(1)}, u32[]{:S(2)}, u32[]{:S(2)}) collective-permute-start(bf16[96,1024]{1,0:T(8,128)(2,1)S(1)} %get-tuple-element.79), channel_id=1, source_target_pairs={{0,24},{4,28},{8,16},{12,20},{16,8},{20,12},{24,0},{28,4},{1,25},{... | collective-permute-start | bytes 589832 | tf_op jit(solution)/shard_map/ppermute | solution.py:207
  42.3 11.9 %collective-permute-start.23 = (bf16[96,1024]{1,0:T(8,128)(2,1)S(1)}, bf16[96,1024]{1,0:T(8,128)(2,1)S(1)}, u32[]{:S(2)}, u32[]{:S(2)}) collective-permute-start(bf16[96,1024]{1,0:T(8,128)(2,1)S(1)} %get-tuple-element.80), channel_id=1, source_target_pairs={{0,28},{4,24},{8,20},{12,16},{16,12},{20,8},{24,4},{28,0},{1,29},{... | collective-permute-start | bytes 589832 | tf_op jit(solution)/shard_map/ppermute | solution.py:207
  45.2 10.8 %collective-permute-start.17 = (bf16[96,1024]{1,0:T(8,128)(2,1)S(1)}, bf16[96,1024]{1,0:T(8,128)(2,1)S(1)}, u32[]{:S(2)}, u32[]{:S(2)}) collective-permute-start(bf16[96,1024]{1,0:T(8,128)(2,1)S(1)} %collective-permute-done.15.refs_0_.refs_8_), channel_id=1, source_target_pairs={{0,2},{1,3},{2,0},{3,1},{4,6},{5,7},{6,4},{7,5},{8,10},{9,11},{10,... | collective-permute-start | bytes 589832 | tf_op jit(solution)/shard_map/ppermute | solution.py:207
  46.9 10.2 %collective-permute-start.18 = (bf16[96,1024]{1,0:T(8,128)(2,1)S(1)}, bf16[96,1024]{1,0:T(8,128)(2,1)S(1)}, u32[]{:S(2)}, u32[]{:S(2)}) collective-permute-start(bf16[96,1024]{1,0:T(8,128)(2,1)S(1)} %collective-permute-done.16.refs_1_.refs_9_), channel_id=1, source_target_pairs={{0,2},{1,3},{2,0},{3,1},{4,6},{5,7},{6,4},{7,5},{8,10},{9,11},{10,... | collective-permute-start | bytes 589832 | tf_op jit(solution)/shard_map/ppermute | solution.py:207
  52.1 21.8 %collective-permute-start.10 = (bf16[784,128]{1,0:T(8,128)(2,1)S(1)}, bf16[784,128]{1,0:T(8,128)(2,1)S(1)}, u32[]{:S(2)}, u32[]{:S(2)}) collective-permute-start(bf16[784,128]{1,0:T(8,128)(2,1)S(1)} %get-tuple-element.66), channel_id=1, source_target_pairs={{0,2},{1,3},{2,0},{3,1},{4,6},{5,7},{6,4},{7,5},{8,10},{9,11},{10,... | collective-permute-start | bytes 602120 | tf_op jit(solution)/shard_map/ppermute | solution.py:207
  53.9 11.8 %collective-permute-start.24 = (bf16[96,1024]{1,0:T(8,128)(2,1)S(1)}, bf16[96,1024]{1,0:T(8,128)(2,1)S(1)}, u32[]{:S(2)}, u32[]{:S(2)}) collective-permute-start(bf16[96,1024]{1,0:T(8,128)(2,1)S(1)} %collective-permute-done.22.refs_0_.refs_12_), channel_id=1, source_target_pairs={{0,2},{1,3},{2,0},{3,1},{4,6},{5,7},{6,4},{7,5},{8,10},{9,11},{10,... | collective-permute-start | bytes 589832 | tf_op jit(solution)/shard_map/ppermute | solution.py:207
  54.2 15.7 %collective-permute-start.25 = (bf16[96,1024]{1,0:T(8,128)(2,1)S(1)}, bf16[96,1024]{1,0:T(8,128)(2,1)S(1)}, u32[]{:S(2)}, u32[]{:S(2)}) collective-permute-start(bf16[96,1024]{1,0:T(8,128)(2,1)S(1)} %collective-permute-done.23.refs_1_.refs_13_), channel_id=1, source_target_pairs={{0,2},{1,3},{2,0},{3,1},{4,6},{5,7},{6,4},{7,5},{8,10},{9,11},{10,... | collective-permute-start | bytes 589832 | tf_op jit(solution)/shard_map/ppermute | solution.py:207
  55.9 18.3 %collective-permute-start.12 = (bf16[784,128]{1,0:T(8,128)(2,1)S(1)}, bf16[784,128]{1,0:T(8,128)(2,1)S(1)}, u32[]{:S(2)}, u32[]{:S(2)}) collective-permute-start(bf16[784,128]{1,0:T(8,128)(2,1)S(1)} %get-tuple-element.70), channel_id=1, source_target_pairs={{0,2},{1,3},{2,0},{3,1},{4,6},{5,7},{6,4},{7,5},{8,10},{9,11},{10,... | collective-permute-start | bytes 602120 | tf_op jit(solution)/shard_map/ppermute | solution.py:207
  59.1 17.4 %collective-permute-start.19 = (bf16[784,128]{1,0:T(8,128)(2,1)S(1)}, bf16[784,128]{1,0:T(8,128)(2,1)S(1)}, u32[]{:S(2)}, u32[]{:S(2)}) collective-permute-start(bf16[784,128]{1,0:T(8,128)(2,1)S(1)} %get-tuple-element.76), channel_id=1, source_target_pairs={{0,2},{1,3},{2,0},{3,1},{4,6},{5,7},{6,4},{7,5},{8,10},{9,11},{10,... | collective-permute-start | bytes 602120 | tf_op jit(solution)/shard_map/ppermute | solution.py:207
  73.3 35.4 %collective-permute-start.29 = (bf16[1024,256]{1,0:T(8,128)(2,1)S(1)}, bf16[1024,256]{1,0:T(8,128)(2,1)S(1)}, u32[]{:S(2)}, u32[]{:S(2)}) collective-permute-start(bf16[1024,256]{1,0:T(8,128)(2,1)S(1)} %get-tuple-element.99), channel_id=1, source_target_pairs={{0,1},{1,0},{2,3},{3,2},{4,5},{5,4},{6,7},{7,6},{8,9},{9,8},{10,11... | collective-permute-start | bytes 1572872 | tf_op jit(solution)/shard_map/ppermute | solution.py:207
  73.4 35.3 %collective-permute-start.30 = (bf16[1024,256]{1,0:T(8,128)(2,1)S(1)}, bf16[1024,256]{1,0:T(8,128)(2,1)S(1)}, u32[]{:S(2)}, u32[]{:S(2)}) collective-permute-start(bf16[1024,256]{1,0:T(8,128)(2,1)S(1)} %get-tuple-element.100), channel_id=1, source_target_pairs={{0,1},{1,0},{2,3},{3,2},{4,5},{5,4},{6,7},{7,6},{8,9},{9,8},{10,11... | collective-permute-start | bytes 1572872 | tf_op jit(solution)/shard_map/ppermute | solution.py:207
  73.9 34.8 %collective-permute-start.31 = (bf16[256,1024]{1,0:T(8,128)(2,1)S(1)}, bf16[256,1024]{1,0:T(8,128)(2,1)S(1)}, u32[]{:S(2)}, u32[]{:S(2)}) collective-permute-start(bf16[256,1024]{1,0:T(8,128)(2,1)S(1)} %get-tuple-element.101), channel_id=1, source_target_pairs={{0,1},{1,0},{2,3},{3,2},{4,5},{5,4},{6,7},{7,6},{8,9},{9,8},{10,11... | collective-permute-start | bytes 1572872 | tf_op jit(solution)/shard_map/ppermute | solution.py:207
  74.2 7.1 %collective-permute-start.26 = (bf16[784,128]{1,0:T(8,128)(2,1)S(1)}, bf16[784,128]{1,0:T(8,128)(2,1)S(1)}, u32[]{:S(2)}, u32[]{:S(2)}) collective-permute-start(bf16[784,128]{1,0:T(8,128)(2,1)S(1)} %get-tuple-element.82), channel_id=1, source_target_pairs={{0,2},{1,3},{2,0},{3,1},{4,6},{5,7},{6,4},{7,5},{8,10},{9,11},{10,... | collective-permute-start | bytes 602120 | tf_op jit(solution)/shard_map/ppermute | solution.py:207
  76.5 4.8 %collective-permute-start.11 = (bf16[392,128]{1,0:T(8,128)(2,1)S(1)}, bf16[392,128]{1,0:T(8,128)(2,1)S(1)}, u32[]{:S(2)}, u32[]{:S(2)}) collective-permute-start(bf16[392,128]{1,0:T(8,128)(2,1)S(1)} %get-tuple-element.68), channel_id=1, source_target_pairs={{0,4},{4,0},{8,12},{12,8},{16,20},{20,16},{24,28},{28,24},{1,5},{5... | collective-permute-start | bytes 301064 | tf_op jit(solution)/shard_map/ppermute | solution.py:207
  81.3 5.2 %collective-permute-start.13 = (bf16[392,128]{1,0:T(8,128)(2,1)S(1)}, bf16[392,128]{1,0:T(8,128)(2,1)S(1)}, u32[]{:S(2)}, u32[]{:S(2)}) collective-permute-start(bf16[392,128]{1,0:T(8,128)(2,1)S(1)} %get-tuple-element.71), channel_id=1, source_target_pairs={{0,8},{4,12},{8,0},{12,4},{16,24},{20,28},{24,16},{28,20},{1,9},{5... | collective-permute-start | bytes 301064 | tf_op jit(solution)/shard_map/ppermute | solution.py:207
  81.3 7.3 %collective-permute-start.14 = (bf16[392,128]{1,0:T(8,128)(2,1)S(1)}, bf16[392,128]{1,0:T(8,128)(2,1)S(1)}, u32[]{:S(2)}, u32[]{:S(2)}) collective-permute-start(bf16[392,128]{1,0:T(8,128)(2,1)S(1)} %get-tuple-element.72), channel_id=1, source_target_pairs={{0,12},{4,8},{8,4},{12,0},{16,28},{20,24},{24,20},{28,16},{1,13},{... | collective-permute-start | bytes 301064 | tf_op jit(solution)/shard_map/ppermute | solution.py:207
  86.4 10.3 %collective-permute-start.20 = (bf16[392,128]{1,0:T(8,128)(2,1)S(1)}, bf16[392,128]{1,0:T(8,128)(2,1)S(1)}, u32[]{:S(2)}, u32[]{:S(2)}) collective-permute-start(bf16[392,128]{1,0:T(8,128)(2,1)S(1)} %get-tuple-element.77), channel_id=1, source_target_pairs={{0,16},{4,20},{8,24},{12,28},{16,0},{20,4},{24,8},{28,12},{1,17},{... | collective-permute-start | bytes 301064 | tf_op jit(solution)/shard_map/ppermute | solution.py:207
  88.6 11.8 %collective-permute-start.21 = (bf16[392,128]{1,0:T(8,128)(2,1)S(1)}, bf16[392,128]{1,0:T(8,128)(2,1)S(1)}, u32[]{:S(2)}, u32[]{:S(2)}) collective-permute-start(bf16[392,128]{1,0:T(8,128)(2,1)S(1)} %get-tuple-element.78), channel_id=1, source_target_pairs={{0,20},{4,16},{8,28},{12,24},{16,4},{20,0},{24,12},{28,8},{1,21},{... | collective-permute-start | bytes 301064 | tf_op jit(solution)/shard_map/ppermute | solution.py:207
  96.8 6.9 %collective-permute-start.27 = (bf16[392,128]{1,0:T(8,128)(2,1)S(1)}, bf16[392,128]{1,0:T(8,128)(2,1)S(1)}, u32[]{:S(2)}, u32[]{:S(2)}) collective-permute-start(bf16[392,128]{1,0:T(8,128)(2,1)S(1)} %get-tuple-element.83), channel_id=1, source_target_pairs={{0,24},{4,28},{8,16},{12,20},{16,8},{20,12},{24,0},{28,4},{1,25},{... | collective-permute-start | bytes 301064 | tf_op jit(solution)/shard_map/ppermute | solution.py:207
  100.3 7.3 %collective-permute-start.28 = (bf16[392,128]{1,0:T(8,128)(2,1)S(1)}, bf16[392,128]{1,0:T(8,128)(2,1)S(1)}, u32[]{:S(2)}, u32[]{:S(2)}) collective-permute-start(bf16[392,128]{1,0:T(8,128)(2,1)S(1)} %get-tuple-element.84), channel_id=1, source_target_pairs={{0,28},{4,24},{8,20},{12,16},{16,12},{20,8},{24,4},{28,0},{1,29},{... | collective-permute-start | bytes 301064 | tf_op jit(solution)/shard_map/ppermute | solution.py:207

commit v2 on v1

--- a/solution.py
+++ b/solution.py
@@ -26,32 +26,42 @@
     return copies
 
 
+def slot_tables(experts, ids, capacity):
+    rows = experts.shape[1]
+    earlier = lax.broadcasted_iota(jnp.int32, (rows, rows), 0) < lax.broadcasted_iota(jnp.int32, (rows, rows), 1)
+    named = (experts[0:1, :] == ids) | (experts[1:2, :] == ids)
+    position = contract(jnp.where(named, 1.0, 0.0).astype(BF16), jnp.where(earlier, 1.0, 0.0).astype(BF16), 1, 0)
+    position = jnp.where(named, position, -1.0)
+    slots = lax.broadcasted_iota(jnp.int32, (capacity, rows), 0).astype(F32)
+    return [slots == position[k : k + 1, :] for k in range(ids.shape[0])]
+
+
+def partner_ids(count, rows, me):
+    return lax.broadcasted_iota(jnp.int32, (count, rows), 0) ^ me
+
+
 def send_kernel(n_experts, capacity, me_ref, *refs):
     sources, refs = refs[:5], refs[5:]
-    (table_ref, exp_out, ratio_out), refs = refs[:3], refs[3:]
+    (table_ref, exp_out, ratio_out, route_out), refs = refs[:4], refs[4:]
     messages, (exp_ref, keep_ref, gate_ref, tok_ref, cot_ref, sems) = refs[:n_experts], refs[n_experts:]
     copies = fetch(sources, (exp_ref, keep_ref, gate_ref, tok_ref, cot_ref), sems)
-    rows = tok_ref.shape[0]
-    earlier = lax.broadcasted_iota(jnp.int32, (rows, rows), 0) < lax.broadcasted_iota(jnp.int32, (rows, rows), 1)
-    ids = lax.broadcasted_iota(jnp.int32, (n_experts, rows), 0) ^ me_ref[0]
+    ids = partner_ids(n_experts, tok_ref.shape[0], me_ref[0])
     for copy in copies[:3]:
         copy.wait()
     gate = gate_ref[...].astype(F32)
     keep = keep_ref[...].astype(F32)
+    experts = exp_ref[...]
     weight = gate * keep
-    exp_out[...] = exp_ref[...]
+    exp_out[...] = experts
     ratio_out[...] = keep / gate
-    named0 = exp_ref[0:1, :] == ids
-    named1 = exp_ref[1:2, :] == ids
-    named = named0 | named1
-    w_of = jnp.where(named0, weight[0:1, :], 0.0) + jnp.where(named1, weight[1:2, :], 0.0)
-    position = contract(jnp.where(named, 1.0, 0.0).astype(BF16), jnp.where(earlier, 1.0, 0.0).astype(BF16), 1, 0)
-    position = jnp.where(named, position, -1.0)
-    slots = lax.broadcasted_iota(jnp.int32, (capacity, rows), 0).astype(F32)
+    route_out[...] = jnp.zeros(route_out.shape, jnp.int32)
+    route_out[0:2, :] = experts
+    w_of = jnp.where(experts[0:1, :] == ids, weight[0:1, :], 0.0)
+    w_of = w_of + jnp.where(experts[1:2, :] == ids, weight[1:2, :], 0.0)
+    hits = slot_tables(experts, ids, capacity)
     for copy in copies[3:]:
         copy.wait()
-    for k in range(n_experts):
-        hit = slots == position[k : k + 1, :]
+    for k, hit in enumerate(hits):
         table = jnp.where(hit, 1.0, 0.0).astype(BF16)
         table_w = jnp.where(hit, w_of[k : k + 1, :], 0.0).astype(BF16)
         table_ref[k * capacity : (k + 1) * capacity, :] = table
@@ -60,8 +70,16 @@
 
 
 def stage_kernel(*refs):
-    for copy in fetch(refs[:3], refs[3:6], refs[6]):
+    sources, (wg_ref, wu_ref), turned, (wd_ref, sems) = refs[:3], refs[3:5], refs[5:8], refs[8:]
+    copies = fetch(sources, (wg_ref, wu_ref, wd_ref), sems)
+    for copy, ref, out in zip(copies, (wg_ref, wu_ref, wd_ref), turned):
         copy.wait()
+        out[...] = ref[...].T
+
+
+def turn_kernel(*refs):
+    for ref, out in zip(refs[:3], refs[3:]):
+        out[...] = ref[...].T
 
 
 def pack(target, m, capacity, values, sums):
@@ -74,21 +92,19 @@
     target[tail, 0:capacity] = sums.astype(BF16)
 
 
-def grad_kernel(n_parts, chunks, capacity, *refs):
-    n_own = sum(chunks)
-    n_msgs = n_parts * n_own
+def grad_kernel(n_msgs, layout, capacity, *refs):
     msgs = refs[:n_msgs]
-    wg_refs, wu_refs, wd_refs = refs[n_msgs : n_msgs + 2], refs[n_msgs + 2 : n_msgs + 4], refs[n_msgs + 4 : n_msgs + 6]
-    outs = refs[n_msgs + 6 :]
+    weights, outs = (refs[n_msgs : n_msgs + 5], refs[n_msgs + 5 : n_msgs + 10]), refs[n_msgs + 10 :]
     back, (da_ref, db_ref, h_ref) = outs[:-3], outs[-3:]
     x = jnp.concatenate([m[0:capacity, :] for m in msgs], axis=0)
     gw = jnp.concatenate([m[capacity:, :] for m in msgs], axis=0)
     part_x = None
     part_g = None
     for q in range(2):
-        a = contract(x, wg_refs[q][...], 1, 0)
-        b = contract(x, wu_refs[q][...], 1, 0)
-        dh = contract(gw, wd_refs[q][...], 1, 1)
+        wg, wu, wg_t, wu_t, wd_t = [ref[...] for ref in weights[q]]
+        a = contract(x, wg, 1, 0)
+        b = contract(x, wu, 1, 0)
+        dh = contract(gw, wd_t, 1, 0)
         sig = 1.0 / (1.0 + jnp.exp(-a))
         act = a * sig
         h = act * b
@@ -99,21 +115,18 @@
         da_ref[:, cols] = da
         db_ref[:, cols] = db
         h_ref[:, cols] = h.astype(BF16)
-        px = contract(da, wg_refs[q][...], 1, 1) + contract(db, wu_refs[q][...], 1, 1)
+        px = contract(da, wg_t, 1, 0) + contract(db, wu_t, 1, 0)
         pg = h * dh
         part_x = px if part_x is None else part_x + px
         part_g = pg if part_g is None else part_g + pg
     high = part_g.astype(BF16)
     low = (part_g - high.astype(F32)).astype(BF16)
     ones = jnp.ones((SUBLANES, part_g.shape[1]), BF16)
-    m = 0
-    for target in [back[p * len(chunks) + c] for p in range(n_parts) for c in range(len(chunks))]:
-        count = target.shape[0] // (part_x.shape[1] // LANES * capacity + SUBLANES)
-        for i in range(count):
+    for target, places in zip(back, layout):
+        for i, m in enumerate(places):
             rows = slice(m * capacity, (m + 1) * capacity)
             sums = contract(ones, high[rows, :], 1, 1) + contract(ones, low[rows, :], 1, 1)
             pack(target, i, capacity, part_x[rows, :], sums)
-            m += 1
 
 
 def weight_kernel(counts, capacity, quarter, *refs):
@@ -148,18 +161,56 @@
         out[...] = total[i * rows : (i + 1) * rows, :].astype(BF16)
 
 
-def combine_kernel(n_experts, capacity, me_ref, exp_ref, ratio_ref, table_ref, *refs):
-    msgs, (dtok_ref, dgate_ref) = refs[:n_experts], refs[n_experts:]
-    blocks = dtok_ref.shape[1] // LANES
-    rows = []
-    for m in msgs:
-        rows.append(jnp.concatenate([m[j * capacity : (j + 1) * capacity, :] for j in range(blocks)], axis=1))
-    dtok_ref[...] = contract(table_ref[...], jnp.concatenate(rows, axis=0), 0, 0).astype(BF16)
-    d_gates = jnp.zeros(exp_ref.shape, F32)
-    for k in range(n_experts):
-        sums = msgs[k][blocks * capacity :, 0:capacity]
-        value = contract(sums, table_ref[k * capacity : (k + 1) * capacity, :], 1, 0)
-        d_gates = d_gates + jnp.where(exp_ref[...] == (me_ref[0] ^ k), value[0 : exp_ref.shape[0], :], 0.0)
+def unpack(messages, part, width, capacity):
+    blocks = width // LANES
+    base = part * (blocks * capacity + SUBLANES)
+    values, sums = [], []
+    for m in messages:
+        cuts = [m[base + j * capacity : base + (j + 1) * capacity, :] for j in range(blocks)]
+        values.append(jnp.concatenate(cuts, axis=1))
+        tail = base + blocks * capacity
+        sums.append(m[tail : tail + SUBLANES, 0:capacity])
+    return jnp.concatenate(values, axis=0), sums
+
+
+def gate_sums(experts, me, first, sums, table, capacity):
+    total = jnp.zeros(experts.shape, F32)
+    for i, row in enumerate(sums):
+        value = contract(row, table[i * capacity : (i + 1) * capacity, :], 1, 0)
+        total = total + jnp.where(experts == (me ^ (first + i)), value[0 : experts.shape[0], :], 0.0)
+    return total
+
+
+def mix_kernel(n_peers, near, capacity, me_ref, exp_ref, table_ref, *refs):
+    routes, refs = refs[:n_peers], refs[n_peers:]
+    messages, (sum_ref, gate_ref), targets = refs[:near], refs[near : near + 2], refs[near + 2 :]
+    rows, width = sum_ref.shape
+    table = table_ref[0 : near * capacity, :]
+    values, sums = unpack(messages, 0, width, capacity)
+    sum_ref[...] = contract(table, values, 0, 0)
+    gate_ref[...] = gate_sums(exp_ref[...], me_ref[0], 0, sums, table, capacity)
+    count = max(near, SUBLANES)
+    for p in range(n_peers):
+        experts = routes[p][0:2, :]
+        hits = slot_tables(experts, partner_ids(count, rows, me_ref[0]), capacity)[:near]
+        table = jnp.concatenate([jnp.where(hit, 1.0, 0.0).astype(BF16) for hit in hits], axis=0)
+        values, sums = unpack(messages, p + 1, width, capacity)
+        targets[p][0:rows, :] = contract(table, values, 0, 0).astype(BF16)
+        targets[p][rows:, :] = jnp.zeros((SUBLANES, width), BF16)
+        targets[p][rows : rows + 2, 0:rows] = gate_sums(experts, me_ref[0], 0, sums, table, capacity).astype(BF16)
+
+
+def combine_kernel(near, n_peers, capacity, me_ref, exp_ref, ratio_ref, table_ref, sum_ref, gate_ref, *refs):
+    parts, messages, (dtok_ref, dgate_ref) = refs[:n_peers], refs[n_peers:-2], refs[-2:]
+    rows, width = dtok_ref.shape
+    table = table_ref[near * capacity :, :]
+    values, sums = unpack(messages, 0, width, capacity)
+    total = sum_ref[...] + contract(table, values, 0, 0)
+    d_gates = gate_ref[...] + gate_sums(exp_ref[...], me_ref[0], near, sums, table, capacity)
+    for part in parts:
+        total = total + part[0:rows, :].astype(F32)
+        d_gates = d_gates + part[rows : rows + 2, 0:rows].astype(F32)
+    dtok_ref[...] = total.astype(BF16)
     dgate_ref[...] = (d_gates * ratio_ref[...]).astype(BF16)
 
 
@@ -180,14 +231,14 @@
     )
 
 
-def chunks_of(n_experts):
+def quarters_of(n_experts):
     size = n_experts // 4
     return [list(range(i * size, (i + 1) * size)) for i in range(4)]
 
 
 def groups_of(n_experts):
-    first, second, third, fourth = chunks_of(n_experts)
-    return [[first, second], [third], [fourth]]
+    first, second, third, fourth = quarters_of(n_experts)
+    return [[first], [second], [third]] + [[[k]] for k in fourth]
 
 
 def local_tiled(tokens, cotangent, gates, experts, keep, gate_w, up_w, down_w):
@@ -212,13 +263,16 @@
     held = [pltpu.with_memory_space_constraint(w[0], pltpu.HBM) for w in (gate_w, up_w, down_w)]
     swapped = [exchange(w[0], "zr", n_groups, 1) for w in (gate_w, up_w, down_w)]
     sems = pltpu.SemaphoreType.DMA
-    held = run(stage_kernel, [w.shape for w in held], *held, hbm=3, scratch=[sems((3,))])
-    weights = [w for pair in zip(held, swapped) for w in pair]
+    turned = [w.shape[::-1] for w in held]
+    scratch = [pltpu.VMEM(held[2].shape, BF16), sems((3,))]
+    held = run(stage_kernel, [w.shape for w in held[:2]] + turned, *held, hbm=3, scratch=scratch)
+    weights = [*held, *swapped[:2], *run(turn_kernel, turned, *swapped)]
 
     inputs = [pltpu.with_memory_space_constraint(v, pltpu.HBM) for v in (*route, tokens, cotangent)]
     outs = [(n_experts * capacity, tok_rows), jax.ShapeDtypeStruct(route[0].shape, jnp.int32)]
-    outs += [jax.ShapeDtypeStruct(route[0].shape, F32)] + [(2 * capacity, width)] * n_experts
-    table, named, ratio, *sends = run(
+    outs += [jax.ShapeDtypeStruct(route[0].shape, F32), jax.ShapeDtypeStruct((SUBLANES, tok_rows), jnp.int32)]
+    outs += [(2 * capacity, width)] * n_experts
+    table, named, ratio, shared, *sends = run(
         functools.partial(send_kernel, n_experts, capacity),
         outs,
         me,
@@ -232,17 +286,27 @@
     theirs = [[exchange(mine[k], "zr", n_groups, r) for r in peers] for k in range(n_experts)]
 
     n_parts = 1 + len(peers)
+    near = n_experts // 2
     msg_rows = width // LANES * capacity + SUBLANES
     all_msgs, counts, das, dbs, hs, returned = [], [], [], [], [], {}
     for chunks in groups_of(n_experts):
         group = sum(chunks, [])
+        n_own = len(group)
         msgs = [mine[k] for k in group] + [theirs[k][p] for p in range(len(peers)) for k in group]
-        outs = [(len(chunk) * msg_rows, LANES) for chunk in chunks] * n_parts
+        if group[0] < near:
+            layout = [[i + p * n_own for p in range(n_parts)] for i in range(n_own)]
+        else:
+            layout = [[group.index(k) + p * n_own for k in chunk] for p in range(n_parts) for chunk in chunks]
+        outs = [(len(places) * msg_rows, LANES) for places in layout]
         outs += [(len(msgs) * capacity, 2 * hidden)] * 3
-        body = functools.partial(grad_kernel, n_parts, [len(chunk) for chunk in chunks], capacity)
+        body = functools.partial(grad_kernel, len(msgs), layout, capacity)
         *back, da, db, h = run(body, outs, *msgs, *weights)
         all_msgs, counts = all_msgs + msgs, counts + [len(msgs)]
         das, dbs, hs = das + [da], dbs + [db], hs + [h]
+        if group[0] < near:
+            for k, value in zip(group, back):
+                returned[k] = exchange(value, "ep", n_experts, k) if k else value
+            continue
         for c, chunk in enumerate(chunks):
             parts = [back[c]]
             for p, r in enumerate(peers):
@@ -250,28 +314,41 @@
             body = functools.partial(sum_kernel, n_parts)
             summed = run(body, [(msg_rows, LANES)] * len(chunk), *parts)
             for k, value in zip(chunk, summed):
-                returned[k] = exchange(value, "ep", n_experts, k) if k else value
+                returned[k] = exchange(value, "ep", n_experts, k)
+
+    found = [exchange(shared, "zr", n_groups, r) for r in peers]
+    outs = [jax.ShapeDtypeStruct((tok_rows, width), F32), jax.ShapeDtypeStruct(named.shape, F32)]
+    outs += [(tok_rows + SUBLANES, width)] * len(peers)
+    near_sum, near_gates, *targets = run(
+        functools.partial(mix_kernel, len(peers), near, capacity),
+        outs,
+        me,
+        named,
+        table,
+        *found,
+        *[returned[k] for k in range(near)],
+        smem=1,
+    )
+    received = [exchange(value, "zr", n_groups, r) for value, r in zip(targets, peers)]
+    near_args = (named, ratio, table, near_sum, near_gates, *received)
 
     shapes = [(width, hidden), (width, hidden), (hidden, width)]
     w_args = all_msgs + das + dbs + hs
     partner = run(functools.partial(weight_kernel, counts, capacity, 1), shapes, *w_args)
-    received = [exchange(w, "zr", n_groups, 1) for w in partner]
+    swapped = [exchange(w, "zr", n_groups, 1) for w in partner]
     own = run(
         functools.partial(weight_kernel, counts, capacity, 0),
         [jax.ShapeDtypeStruct(shape, F32) for shape in shapes],
         *w_args,
     )
-    dwg, dwu, dwd = run(add_kernel, shapes, *own, *received)
-
-    outs = [(tok_rows, width), experts.T.shape]
+    dwg, dwu, dwd = run(add_kernel, shapes, *own, *swapped)
+
     d_tokens, d_gates = run(
-        functools.partial(combine_kernel, n_experts, capacity),
-        outs,
+        functools.partial(combine_kernel, near, len(peers), capacity),
+        [(tok_rows, width), named.shape],
         me,
-        named,
-        ratio,
-        table,
-        *[returned[k] for k in range(n_experts)],
+        *near_args,
+        *[returned[k] for k in range(near, n_experts)],
         smem=1,
     )
     return d_tokens, d_gates.T, dwg[None], dwu[None], dwd[None]
@@ -389,7 +466,9 @@
 def tiled(mesh, tokens):
     n_experts, n_groups = mesh.shape["ep"], mesh.shape["zr"]
     capacity = 3 * (tokens.shape[0] // (n_experts * n_groups)) // n_experts
-    return paired(mesh) and capacity % 16 == 0 and tokens.shape[1] % LANES == 0
+    rows, width = tokens.shape[0] // (n_experts * n_groups), tokens.shape[1]
+    aligned = capacity % 16 == 0 and capacity <= LANES and rows % 16 == 0 and rows <= width and width % LANES == 0
+    return paired(mesh) and aligned
 
 
 def solution(mesh):

time: 110 us -> 116 us (1.055)
  starting transfers between devices: 41.3 us -> 55.3 us
  waiting for transfers between devices: 51.9 us -> 41 us
  Pallas kernels: 16.1 us -> 18.6 us
    ppermute x32 -> x33, starting transfers between devices: 41.3 us -> 55.3 us  [exchange(): return lax.ppermute(value, axis, [(i, i ^ bit) for i in range(size)])]
    ppermute x32 -> x33, waiting for transfers between devices: 51.9 us -> 41 us  [exchange(): return lax.ppermute(value, axis, [(i, i ^ bit) for i in range(size)])]
    pallas_call x13 -> x16, Pallas kernels: 16.1 us -> 18.6 us  [run(): return call(body, outs, len(args), **kinds)(*args)]
  transfers between devices with their start and end apart: 32 -> 33, of which waited for: 16 -> 13; matrix products, arithmetic and copies ran while one was open for 0% -> 0% of each run, Pallas kernels for 12% -> 13%
where the time goes in v2:
time: 116 us
  starting transfers between devices  55.3 us (48%)
  waiting for transfers between devices  41 us (35%)
  Pallas kernels  18.6 us (16%)
    ppermute x33, starting transfers between devices, exchange(): return lax.ppermute(value, axis, [(i, i ^ bit) for i in range(size)])  55.3 us
    ppermute x33, waiting for transfers between devices, exchange(): return lax.ppermute(value, axis, [(i, i ^ bit) for i in range(size)])  41 us
    pallas_call x16, Pallas kernels, run(): return call(body, outs, len(args), **kinds)(*args)  18.6 us
  transfers between devices with their start and end apart: 33, of which 13 were waited for; matrix products, arithmetic and copies ran while one was open for 0% of the time, Pallas kernels for 13%

profile of v2, /device:TPU:0, one launch (start us, length us, event | category | flops | bytes accessed | tf_op | source)
XLA Modules:
  0.0 115.7 jit_solution(360517172417650453)
XLA Ops:
  0.6 0.0 copy-start
  0.6 1.9 %shard_map.119 = (bf16[384,128]{1,0:T(8,128)(2,1)S(1)}, s32[2,128]{1,0:T(2,128)S(1)}, f32[2,128]{1,0:T(2,128)S(1)}, s32[8,128]{1,0:T(8,128)S(1)}, bf16[96,1024]{...) custom-call(s32[1]{0:T(128)} %bitcast.me_ref, ...), custom_call_target="tpu_custom_call" | custom-call | tf_op jit(solution)/shard_map/pallas_call | solution.py:261
  2.6 3.1 %collective-permute-start.1 = (bf16[96,1024]{1,0:T(8,128)(2,1)S(1)}, bf16[96,1024]{1,0:T(8,128)(2,1)S(1)}, u32[]{:S(2)}, u32[]{:S(2)}) collective-permute-start(bf16[96,1024]{1,0:T(8,128)(2,1)S(1)} %get-tuple-element.71), channel_id=1, source_target_pairs={{0,4},{4,0},{8,12},{12,8},{16,20},{20,16},{24,28},{28,24},{1,5},{5... | collective-permute-start | bytes 589832 | tf_op jit(solution)/shard_map/ppermute | solution.py:258
  5.6 1.6 %collective-permute-start.8 = (bf16[96,1024]{1,0:T(8,128)(2,1)S(1)}, bf16[96,1024]{1,0:T(8,128)(2,1)S(1)}, u32[]{:S(2)}, u32[]{:S(2)}) collective-permute-start(bf16[96,1024]{1,0:T(8,128)(2,1)S(1)} %get-tuple-element.82), channel_id=1, source_target_pairs={{0,8},{4,12},{8,0},{12,4},{16,24},{20,28},{24,16},{28,20},{1,9},{5... | collective-permute-start | bytes 589832 | tf_op jit(solution)/shard_map/ppermute | solution.py:258
  7.2 0.0 collective-permute-start.9
  7.2 3.0 %collective-permute-start.15 = (bf16[96,1024]{1,0:T(8,128)(2,1)S(1)}, bf16[96,1024]{1,0:T(8,128)(2,1)S(1)}, u32[]{:S(2)}, u32[]{:S(2)}) collective-permute-start(bf16[96,1024]{1,0:T(8,128)(2,1)S(1)} %get-tuple-element.89), channel_id=1, source_target_pairs={{0,16},{4,20},{8,24},{12,28},{16,0},{20,4},{24,8},{28,12},{1,17},{... | collective-permute-start | bytes 589832 | tf_op jit(solution)/shard_map/ppermute | solution.py:258
  10.2 1.3 %collective-permute-start.16 = (bf16[96,1024]{1,0:T(8,128)(2,1)S(1)}, bf16[96,1024]{1,0:T(8,128)(2,1)S(1)}, u32[]{:S(2)}, u32[]{:S(2)}) collective-permute-start(bf16[96,1024]{1,0:T(8,128)(2,1)S(1)} %get-tuple-element.90), channel_id=1, source_target_pairs={{0,20},{4,16},{8,28},{12,24},{16,4},{20,0},{24,12},{28,8},{1,21},{... | collective-permute-start | bytes 589832 | tf_op jit(solution)/shard_map/ppermute | solution.py:258
  11.5 0.0 collective-permute-done.1.refs_1_
  11.5 10.2 %collective-permute-done.8.refs_0_.refs_4_ = bf16[96,1024]{1,0:T(8,128)(2,1)S(1)} collective-permute-done((bf16[96,1024]{1,0:T(8,128)(2,1)S(1)}, bf16[96,1024]{1,0:T(8,128)(2,1)S(1)}, u32[]{:S(2)}, u32[]{:S(2)}) %collective-permute-start.8) | collective-permute-done | bytes 196640 | tf_op jit(solution)/shard_map/ppermute | solution.py:258
  21.6 0.0 collective-permute-start.5
  21.6 1.5 %collective-permute-done.9.refs_1_.refs_5_ = bf16[96,1024]{1,0:T(8,128)(2,1)S(1)} collective-permute-done((bf16[96,1024]{1,0:T(8,128)(2,1)S(1)}, bf16[96,1024]{1,0:T(8,128)(2,1)S(1)}, u32[]{:S(2)}, u32[]{:S(2)}) %collective-permute-start.9) | collective-permute-done | bytes 196640 | tf_op jit(solution)/shard_map/ppermute | solution.py:258
  23.2 5.1 %collective-permute-start.22 = (bf16[96,1024]{1,0:T(8,128)(2,1)S(1)}, bf16[96,1024]{1,0:T(8,128)(2,1)S(1)}, u32[]{:S(2)}, u32[]{:S(2)}) collective-permute-start(bf16[96,1024]{1,0:T(8,128)(2,1)S(1)} %get-tuple-element.95), channel_id=1, source_target_pairs={{0,24},{4,28},{8,16},{12,20},{16,8},{20,12},{24,0},{28,4},{1,25},{... | collective-permute-start | bytes 589832 | tf_op jit(solution)/shard_map/ppermute | solution.py:258
  28.3 0.9 collective-permute-done.16.refs_1_.refs_9_
  29.2 10.5 %collective-permute-start.26 = (bf16[96,1024]{1,0:T(8,128)(2,1)S(1)}, bf16[96,1024]{1,0:T(8,128)(2,1)S(1)}, u32[]{:S(2)}, u32[]{:S(2)}) collective-permute-start(bf16[96,1024]{1,0:T(8,128)(2,1)S(1)} %get-tuple-element.98), channel_id=1, source_target_pairs={{0,28},{4,24},{8,20},{12,16},{16,12},{20,8},{24,4},{28,0},{1,29},{... | collective-permute-start | bytes 589832 | tf_op jit(solution)/shard_map/ppermute | solution.py:258
  39.7 0.0 collective-permute-done.22.refs_0_.refs_12_
  39.7 1.5 %collective-permute-start.2 = (bf16[96,1024]{1,0:T(8,128)(2,1)S(1)}, bf16[96,1024]{1,0:T(8,128)(2,1)S(1)}, u32[]{:S(2)}, u32[]{:S(2)}) collective-permute-start(bf16[96,1024]{1,0:T(8,128)(2,1)S(1)} %get-tuple-element.70.refs_0_), channel_id=1, source_target_pairs={{0,2},{1,3},{2,0},{3,1},{4,6},{5,7},{6,4},{7,5},{8,10},{9,11},{10,... | collective-permute-start | bytes 589832 | tf_op jit(solution)/shard_map/ppermute | solution.py:258
  41.2 2.3 %collective-permute-done.26.refs_0_.refs_14_ = bf16[96,1024]{1,0:T(8,128)(2,1)S(1)} collective-permute-done((bf16[96,1024]{1,0:T(8,128)(2,1)S(1)}, bf16[96,1024]{1,0:T(8,128)(2,1)S(1)}, u32[]{:S(2)}, u32[]{:S(2)}) %collective-permute-start.26) | collective-permute-done | bytes 196640 | tf_op jit(solution)/shard_map/ppermute | solution.py:258
  43.5 1.5 %collective-permute-start.27 = (bf16[96,1024]{1,0:T(8,128)(2,1)S(1)}, bf16[96,1024]{1,0:T(8,128)(2,1)S(1)}, u32[]{:S(2)}, u32[]{:S(2)}) collective-permute-start(bf16[96,1024]{1,0:T(8,128)(2,1)S(1)} %collective-permute-done.26.refs_0_.refs_14_), channel_id=1, source_target_pairs={{0,2},{1,3},{2,0},{3,1},{4,6},{5,7},{6,4},{7,5},{8,10},{9,11},{10,... | collective-permute-start | bytes 589832 | tf_op jit(solution)/shard_map/ppermute | solution.py:258
  45.0 2.2 %collective-permute-done.2.refs_2_ = bf16[96,1024]{1,0:T(8,128)(2,1)S(1)} collective-permute-done((bf16[96,1024]{1,0:T(8,128)(2,1)S(1)}, bf16[96,1024]{1,0:T(8,128)(2,1)S(1)}, u32[]{:S(2)}, u32[]{:S(2)}) %collective-permute-start.2) | collective-permute-done | bytes 196640 | tf_op jit(solution)/shard_map/ppermute | solution.py:258
  47.2 1.5 %collective-permute-start.10 = (bf16[96,1024]{1,0:T(8,128)(2,1)S(1)}, bf16[96,1024]{1,0:T(8,128)(2,1)S(1)}, u32[]{:S(2)}, u32[]{:S(2)}) collective-permute-start(bf16[96,1024]{1,0:T(8,128)(2,1)S(1)} %collective-permute-done.8.refs_0_.refs_4_), channel_id=1, source_target_pairs={{0,2},{1,3},{2,0},{3,1},{4,6},{5,7},{6,4},{7,5},{8,10},{9,11},{10,... | collective-permute-start | bytes 589832 | tf_op jit(solution)/shard_map/ppermute | solution.py:258
  48.7 2.7 %collective-permute-done.27.refs_1_.refs_15_ = bf16[96,1024]{1,0:T(8,128)(2,1)S(1)} collective-permute-done((bf16[96,1024]{1,0:T(8,128)(2,1)S(1)}, bf16[96,1024]{1,0:T(8,128)(2,1)S(1)}, u32[]{:S(2)}, u32[]{:S(2)}) %collective-permute-start.27) | collective-permute-done | bytes 196640 | tf_op jit(solution)/shard_map/ppermute | solution.py:258
  51.4 1.5 %collective-permute-start.11 = (bf16[96,1024]{1,0:T(8,128)(2,1)S(1)}, bf16[96,1024]{1,0:T(8,128)(2,1)S(1)}, u32[]{:S(2)}, u32[]{:S(2)}) collective-permute-start(bf16[96,1024]{1,0:T(8,128)(2,1)S(1)} %collective-permute-done.9.refs_1_.refs_5_), channel_id=1, source_target_pairs={{0,2},{1,3},{2,0},{3,1},{4,6},{5,7},{6,4},{7,5},{8,10},{9,11},{10,... | collective-permute-start | bytes 589832 | tf_op jit(solution)/shard_map/ppermute | solution.py:258
  52.9 0.5 collective-permute-start.3
  53.5 1.5 %collective-permute-start.23 = (bf16[96,1024]{1,0:T(8,128)(2,1)S(1)}, bf16[96,1024]{1,0:T(8,128)(2,1)S(1)}, u32[]{:S(2)}, u32[]{:S(2)}) collective-permute-start(bf16[96,1024]{1,0:T(8,128)(2,1)S(1)} %collective-permute-done.22.refs_0_.refs_12_), channel_id=1, source_target_pairs={{0,2},{1,3},{2,0},{3,1},{4,6},{5,7},{6,4},{7,5},{8,10},{9,11},{10,... | collective-permute-start | bytes 589832 | tf_op jit(solution)/shard_map/ppermute | solution.py:258
  55.0 0.0 collective-permute-done.6.refs_2_
  55.0 0.5 collective-permute-start.17
  55.5 1.7 %shard_map.120 = (bf16[1024,256]{1,0:T(8,128)(2,1)S(1)}, bf16[1024,256]{1,0:T(8,128)(2,1)S(1)}, bf16[256,1024]{1,0:T(8,128)(2,1)S(1)}, bf16[256,1024]{1,0:T(8,128)(2,1)S(1)}, bf16[1024,256]{1,0:T(8,128)(2,1)S(1)}) custom-call(bf16[1024,256]{1,0:T(8,128)(2,1)} %bitcast.11, bf16[1024,256]{1,0:T(8,128)(2,1)} %bitcast.14, bf16[256,1024]{1,0:T(8,128)(2,1)} %bitcast.16), custom_call_target="tpu_custom_call" | custom-call | tf_op jit(solution)/shard_map/pallas_call | solution.py:261
  57.1 0.5 shard_map.121
  57.6 1.4 %shard_map.129 = (bf16[392,128]{1,0:T(8,128)(2,1)S(1)}, bf16[392,128]{1,0:T(8,128)(2,1)S(1)}, bf16[96,512]{1,0:T(8,128)(2,1)S(1)}, bf16[96,512]{1,0:T(8,128)(2,1)S(1)}, bf16[96,512]{1,0:T(8,128)(2,1)S(1)}) custom-call(bf16[96,1024]{1,0:T(8,128)(2,1)S(1)} %collective-permute-done.26.refs_0_.refs_14_, ...), custom_call_target="tpu_custom_call" | custom-call | tf_op jit(solution)/shard_map/pallas_call | solution.py:261
  59.1 0.0 collective-permute-done.10.refs_2_.refs_6_
  59.1 1.6 %collective-permute-start.18 = (bf16[96,1024]{1,0:T(8,128)(2,1)S(1)}, bf16[96,1024]{1,0:T(8,128)(2,1)S(1)}, u32[]{:S(2)}, u32[]{:S(2)}) collective-permute-start(bf16[96,1024]{1,0:T(8,128)(2,1)S(1)} %collective-permute-done.16.refs_1_.refs_9_), channel_id=1, source_target_pairs={{0,2},{1,3},{2,0},{3,1},{4,6},{5,7},{6,4},{7,5},{8,10},{9,11},{10,... | collective-permute-start | bytes 589832 | tf_op jit(solution)/shard_map/ppermute | solution.py:258
  60.7 0.7 collective-permute-start.28
  61.4 2.0 %shard_map.123 = (bf16[784,128]{1,0:T(8,128)(2,1)S(1)}, bf16[784,128]{1,0:T(8,128)(2,1)S(1)}, bf16[192,512]{1,0:T(8,128)(2,1)S(1)}, bf16[192,512]{1,0:T(8,128)(2,1)S(1)}, bf16[192,512]{1,0:T(8,128)(2,1)S(1)}) custom-call(bf16[96,1024]{1,0:T(8,128)(2,1)S(1)} %collective-permute-done.8.refs_0_.refs_4_, ...), custom_call_target="tpu_custom_call" | custom-call | tf_op jit(solution)/shard_map/pallas_call | solution.py:261
  63.3 0.7 collective-permute-done.3.refs_3_
  64.1 1.7 %collective-permute-start.12 = (bf16[784,128]{1,0:T(8,128)(2,1)S(1)}, bf16[784,128]{1,0:T(8,128)(2,1)S(1)}, u32[]{:S(2)}, u32[]{:S(2)}) collective-permute-start(bf16[784,128]{1,0:T(8,128)(2,1)S(1)} %get-tuple-element.84), channel_id=1, source_target_pairs={{0,8},{4,12},{8,0},{12,4},{16,24},{20,28},{24,16},{28,20},{1,9},{5... | collective-permute-start | bytes 602120 | tf_op jit(solution)/shard_map/ppermute | solution.py:258
  65.8 1.8 %collective-permute-done.23.refs_1_.refs_13_ = bf16[96,1024]{1,0:T(8,128)(2,1)S(1)} collective-permute-done((bf16[96,1024]{1,0:T(8,128)(2,1)S(1)}, bf16[96,1024]{1,0:T(8,128)(2,1)S(1)}, u32[]{:S(2)}, u32[]{:S(2)}) %collective-permute-start.23) | collective-permute-done | bytes 196640 | tf_op jit(solution)/shard_map/ppermute | solution.py:258
  67.6 2.7 %collective-permute-start.13 = (bf16[784,128]{1,0:T(8,128)(2,1)S(1)}, bf16[784,128]{1,0:T(8,128)(2,1)S(1)}, u32[]{:S(2)}, u32[]{:S(2)}) collective-permute-start(bf16[784,128]{1,0:T(8,128)(2,1)S(1)} %get-tuple-element.85), channel_id=1, source_target_pairs={{0,12},{4,8},{8,4},{12,0},{16,28},{20,24},{24,20},{28,16},{1,13},{... | collective-permute-start | bytes 602120 | tf_op jit(solution)/shard_map/ppermute | solution.py:258
  70.3 1.4 %shard_map.127 = (bf16[392,128]{1,0:T(8,128)(2,1)S(1)}, bf16[392,128]{1,0:T(8,128)(2,1)S(1)}, bf16[96,512]{1,0:T(8,128)(2,1)S(1)}, bf16[96,512]{1,0:T(8,128)(2,1)S(1)}, bf16[96,512]{1,0:T(8,128)(2,1)S(1)}) custom-call(bf16[96,1024]{1,0:T(8,128)(2,1)S(1)} %collective-permute-done.22.refs_0_.refs_12_, ...), custom_call_target="tpu_custom_call" | custom-call | tf_op jit(solution)/shard_map/pallas_call | solution.py:261
  71.7 2.3 %collective-permute-done.28.refs_1_ = bf16[392,128]{1,0:T(8,128)(2,1)S(1)} collective-permute-done((bf16[392,128]{1,0:T(8,128)(2,1)S(1)}, bf16[392,128]{1,0:T(8,128)(2,1)S(1)}, u32[]{:S(2)}, u32[]{:S(2)}) %collective-permute-start.28) | collective-permute-done | bytes 100384 | tf_op jit(solution)/shard_map/ppermute | solution.py:258
  74.0 1.5 %collective-permute-start.24 = (bf16[392,128]{1,0:T(8,128)(2,1)S(1)}, bf16[392,128]{1,0:T(8,128)(2,1)S(1)}, u32[]{:S(2)}, u32[]{:S(2)}) collective-permute-start(bf16[392,128]{1,0:T(8,128)(2,1)S(1)} %get-tuple-element.97), channel_id=1, source_target_pairs={{0,2},{1,3},{2,0},{3,1},{4,6},{5,7},{6,4},{7,5},{8,10},{9,11},{10,... | collective-permute-start | bytes 301064 | tf_op jit(solution)/shard_map/ppermute | solution.py:258
  75.5 0.0 collective-permute-done.17.refs_2_.refs_10_
  75.5 2.3 %collective-permute-start.29 = (bf16[392,128]{1,0:T(8,128)(2,1)S(1)}, bf16[392,128]{1,0:T(8,128)(2,1)S(1)}, u32[]{:S(2)}, u32[]{:S(2)}) collective-permute-start(bf16[392,128]{1,0:T(8,128)(2,1)S(1)} %shard_map.130), channel_id=1, source_target_pairs={{0,28},{4,24},{8,20},{12,16},{16,12},{20,8},{24,4},{28,0},{1,29},{... | collective-permute-start | bytes 301064 | tf_op jit(solution)/shard_map/ppermute | solution.py:258
  77.8 0.5 collective-permute-start
  78.3 2.0 %shard_map.125 = (bf16[784,128]{1,0:T(8,128)(2,1)S(1)}, bf16[784,128]{1,0:T(8,128)(2,1)S(1)}, bf16[192,512]{1,0:T(8,128)(2,1)S(1)}, bf16[192,512]{1,0:T(8,128)(2,1)S(1)}, bf16[192,512]{1,0:T(8,128)(2,1)S(1)}) custom-call(bf16[96,1024]{1,0:T(8,128)(2,1)S(1)} %collective-permute-done.15.refs_0_.refs_8_, ...), custom_call_target="tpu_custom_call" | custom-call | tf_op jit(solution)/shard_map/pallas_call | solution.py:261
  80.2 2.0 %shard_map.122 = (bf16[784,128]{1,0:T(8,128)(2,1)S(1)}, bf16[784,128]{1,0:T(8,128)(2,1)S(1)}, bf16[192,512]{1,0:T(8,128)(2,1)S(1)}, bf16[192,512]{1,0:T(8,128)(2,1)S(1)}, bf16[192,512]{1,0:T(8,128)(2,1)S(1)}) custom-call(bf16[96,1024]{1,0:T(8,128)(2,1)S(1)} %get-tuple-element.70.refs_0_, bf16[96,1024]{1,0:T(8,128)(2,1)S(1)} %collective-permute-done.1.refs_1_, ...), custom_call_target="tpu_custom_call" | custom-call | tf_op jit(solution)/shard_map/pallas_call | solution.py:261
  82.2 1.4 %shard_map.133 = (bf16[1024,256]{1,0:T(8,128)(2,1)S(1)}, bf16[1024,256]{1,0:T(8,128)(2,1)S(1)}, bf16[256,1024]{1,0:T(8,128)(2,1)S(1)}) custom-call(bf16[96,1024]{1,0:T(8,128)(2,1)S(1)} %get-tuple-element.70.refs_0_, bf16[96,1024]{1,0:T(8,128)(2,1)S(1)} %collective-permute-done.1.refs_1_, bf16[96,1024]{1,0:T(8,128)(2,1)S(1)} %collective-permute-done.2.refs_2_, ...), custom_call_target="tpu_custom_call" | custom-call | tf_op jit(solution)/shard_map/pallas_call | solution.py:261
  83.7 0.1 collective-permute-start.30
  83.8 0.5 collective-permute-start.31
  84.3 0.1 collective-permute-start.32
  84.3 1.5 %collective-permute-start.7 = (bf16[784,128]{1,0:T(8,128)(2,1)S(1)}, bf16[784,128]{1,0:T(8,128)(2,1)S(1)}, u32[]{:S(2)}, u32[]{:S(2)}) collective-permute-start(bf16[784,128]{1,0:T(8,128)(2,1)S(1)} %get-tuple-element.81), channel_id=1, source_target_pairs={{0,4},{4,0},{8,12},{12,8},{16,20},{20,16},{24,28},{28,24},{1,5},{5... | collective-permute-start | bytes 602120 | tf_op jit(solution)/shard_map/ppermute | solution.py:258
  85.9 1.5 %collective-permute-start.19 = (bf16[784,128]{1,0:T(8,128)(2,1)S(1)}, bf16[784,128]{1,0:T(8,128)(2,1)S(1)}, u32[]{:S(2)}, u32[]{:S(2)}) collective-permute-start(bf16[784,128]{1,0:T(8,128)(2,1)S(1)} %get-tuple-element.92), channel_id=1, source_target_pairs={{0,2},{1,3},{2,0},{3,1},{4,6},{5,7},{6,4},{7,5},{8,10},{9,11},{10,... | collective-permute-start | bytes 602120 | tf_op jit(solution)/shard_map/ppermute | solution.py:258
  87.4 4.3 %collective-permute-done.7.refs_2_ = bf16[784,128]{1,0:T(8,128)(2,1)S(1)} collective-permute-done((bf16[784,128]{1,0:T(8,128)(2,1)S(1)}, bf16[784,128]{1,0:T(8,128)(2,1)S(1)}, u32[]{:S(2)}, u32[]{:S(2)}) %collective-permute-start.7) | collective-permute-done | bytes 200736 | tf_op jit(solution)/shard_map/ppermute | solution.py:258
  91.7 1.6 %collective-permute-start.25 = (bf16[392,128]{1,0:T(8,128)(2,1)S(1)}, bf16[392,128]{1,0:T(8,128)(2,1)S(1)}, u32[]{:S(2)}, u32[]{:S(2)}) collective-permute-start(bf16[392,128]{1,0:T(8,128)(2,1)S(1)} %shard_map.128), channel_id=1, source_target_pairs={{0,24},{4,28},{8,16},{12,20},{16,8},{20,12},{24,0},{28,4},{1,25},{... | collective-permute-start | bytes 301064 | tf_op jit(solution)/shard_map/ppermute | solution.py:258
  93.3 0.5 shard_map.124
  93.9 1.5 %collective-permute-start.14 = (bf16[136,1024]{1,0:T(8,128)(2,1)S(1)}, bf16[136,1024]{1,0:T(8,128)(2,1)S(1)}, u32[]{:S(2)}, u32[]{:S(2)}) collective-permute-start(bf16[136,1024]{1,0:T(8,128)(2,1)S(1)} %get-tuple-element.88), channel_id=1, source_target_pairs={{0,2},{1,3},{2,0},{3,1},{4,6},{5,7},{6,4},{7,5},{8,10},{9,11},{10,... | collective-permute-start | bytes 835592 | tf_op jit(solution)/shard_map/ppermute | solution.py:258
  95.3 0.1 shard_map.126
  95.4 2.8 %collective-permute-done.25.refs_3_ = bf16[392,128]{1,0:T(8,128)(2,1)S(1)} collective-permute-done((bf16[392,128]{1,0:T(8,128)(2,1)S(1)}, bf16[392,128]{1,0:T(8,128)(2,1)S(1)}, u32[]{:S(2)}, u32[]{:S(2)}) %collective-permute-start.25) | collective-permute-done | bytes 100384 | tf_op jit(solution)/shard_map/ppermute | solution.py:258
  98.2 2.8 %collective-permute-start.20 = (bf16[392,128]{1,0:T(8,128)(2,1)S(1)}, bf16[392,128]{1,0:T(8,128)(2,1)S(1)}, u32[]{:S(2)}, u32[]{:S(2)}) collective-permute-start(bf16[392,128]{1,0:T(8,128)(2,1)S(1)} %get-tuple-element.93), channel_id=1, source_target_pairs={{0,16},{4,20},{8,24},{12,28},{16,0},{20,4},{24,8},{28,12},{1,17},{... | collective-permute-start | bytes 301064 | tf_op jit(solution)/shard_map/ppermute | solution.py:258
  101.0 5.0 %collective-permute-done.20.refs_1_ = bf16[392,128]{1,0:T(8,128)(2,1)S(1)} collective-permute-done((bf16[392,128]{1,0:T(8,128)(2,1)S(1)}, bf16[392,128]{1,0:T(8,128)(2,1)S(1)}, u32[]{:S(2)}, u32[]{:S(2)}) %collective-permute-start.20) | collective-permute-done | bytes 100384 | tf_op jit(solution)/shard_map/ppermute | solution.py:258
  106.0 1.6 %collective-permute-start.21 = (bf16[392,128]{1,0:T(8,128)(2,1)S(1)}, bf16[392,128]{1,0:T(8,128)(2,1)S(1)}, u32[]{:S(2)}, u32[]{:S(2)}) collective-permute-start(bf16[392,128]{1,0:T(8,128)(2,1)S(1)} %get-tuple-element.94), channel_id=1, source_target_pairs={{0,20},{4,16},{8,28},{12,24},{16,4},{20,0},{24,12},{28,8},{1,21},{... | collective-permute-start | bytes 301064 | tf_op jit(solution)/shard_map/ppermute | solution.py:258
  107.5 1.4 %shard_map.132 = (f32[1024,256]{1,0:T(8,128)S(1)}, f32[1024,256]{1,0:T(8,128)S(1)}, f32[256,1024]{1,0:T(8,128)S(1)}) custom-call(bf16[96,1024]{1,0:T(8,128)(2,1)S(1)} %get-tuple-element.70.refs_0_, bf16[96,1024]{1,0:T(8,128)(2,1)S(1)} %collective-permute-done.1.refs_1_, bf16[96,1024]{1,0:T(8,128)(2,1)S(1)} %collective-permute-done.2.refs_2_, ...), custom_call_target="tpu_custom_call" | custom-call | tf_op jit(solution)/shard_map/pallas_call | solution.py:261
  108.9 4.5 %collective-permute-done.21.refs_2_ = bf16[392,128]{1,0:T(8,128)(2,1)S(1)} collective-permute-done((bf16[392,128]{1,0:T(8,128)(2,1)S(1)}, bf16[392,128]{1,0:T(8,128)(2,1)S(1)}, u32[]{:S(2)}, u32[]{:S(2)}) %collective-permute-start.21) | collective-permute-done | bytes 100384 | tf_op jit(solution)/shard_map/ppermute | solution.py:258
  113.4 1.0 shard_map.131
  114.4 1.3 %shard_map.134 = (bf16[1024,256]{1,0:T(8,128)(2,1)}, bf16[1024,256]{1,0:T(8,128)(2,1)}, bf16[256,1024]{1,0:T(8,128)(2,1)}) custom-call(f32[1024,256]{1,0:T(8,128)S(1)} %get-tuple-element.118.refs_0_, f32[1024,256]{1,0:T(8,128)S(1)} %get-tuple-element.119.refs_1_, f32[256,1024]{1,0:T(8,128)S(1)} %get-tuple-element.120.refs_2_, ...), custom_call_target="tpu_custom_call" | custom-call | tf_op jit(solution)/shard_map/pallas_call | solution.py:261
  (20 shorter events, 0.1 us)
Async XLA Ops:
  0.6 10.8 %copy-start = (bf16[1,1024,256]{2,1,0:T(8,128)(2,1)S(1)}, bf16[1,1024,256]{2,1,0:T(8,128)(2,1)}, u32[]{:S(2)}) copy-start(bf16[1,1024,256]{2,1,0:T(8,128)(2,1)} %param.13) | copy-start | bytes 1572868
  2.6 8.9 %collective-permute-start.1 = (bf16[96,1024]{1,0:T(8,128)(2,1)S(1)}, bf16[96,1024]{1,0:T(8,128)(2,1)S(1)}, u32[]{:S(2)}, u32[]{:S(2)}) collective-permute-start(bf16[96,1024]{1,0:T(8,128)(2,1)S(1)} %get-tuple-element.71), channel_id=1, source_target_pairs={{0,4},{4,0},{8,12},{12,8},{16,20},{20,16},{24,28},{28,24},{1,5},{5... | collective-permute-start | bytes 589832 | tf_op jit(solution)/shard_map/ppermute | solution.py:258
  5.6 16.0 %collective-permute-start.8 = (bf16[96,1024]{1,0:T(8,128)(2,1)S(1)}, bf16[96,1024]{1,0:T(8,128)(2,1)S(1)}, u32[]{:S(2)}, u32[]{:S(2)}) collective-permute-start(bf16[96,1024]{1,0:T(8,128)(2,1)S(1)} %get-tuple-element.82), channel_id=1, source_target_pairs={{0,8},{4,12},{8,0},{12,4},{16,24},{20,28},{24,16},{28,20},{1,9},{5... | collective-permute-start | bytes 589832 | tf_op jit(solution)/shard_map/ppermute | solution.py:258
  7.2 16.0 %collective-permute-start.9 = (bf16[96,1024]{1,0:T(8,128)(2,1)S(1)}, bf16[96,1024]{1,0:T(8,128)(2,1)S(1)}, u32[]{:S(2)}, u32[]{:S(2)}) collective-permute-start(bf16[96,1024]{1,0:T(8,128)(2,1)S(1)} %get-tuple-element.83), channel_id=1, source_target_pairs={{0,12},{4,8},{8,4},{12,0},{16,28},{20,24},{24,20},{28,16},{1,13},{... | collective-permute-start | bytes 589832 | tf_op jit(solution)/shard_map/ppermute | solution.py:258
  7.2 16.0 %collective-permute-start.15 = (bf16[96,1024]{1,0:T(8,128)(2,1)S(1)}, bf16[96,1024]{1,0:T(8,128)(2,1)S(1)}, u32[]{:S(2)}, u32[]{:S(2)}) collective-permute-start(bf16[96,1024]{1,0:T(8,128)(2,1)S(1)} %get-tuple-element.89), channel_id=1, source_target_pairs={{0,16},{4,20},{8,24},{12,28},{16,0},{20,4},{24,8},{28,12},{1,17},{... | collective-permute-start | bytes 589832 | tf_op jit(solution)/shard_map/ppermute | solution.py:258
  10.2 19.0 %collective-permute-start.16 = (bf16[96,1024]{1,0:T(8,128)(2,1)S(1)}, bf16[96,1024]{1,0:T(8,128)(2,1)S(1)}, u32[]{:S(2)}, u32[]{:S(2)}) collective-permute-start(bf16[96,1024]{1,0:T(8,128)(2,1)S(1)} %get-tuple-element.90), channel_id=1, source_target_pairs={{0,20},{4,16},{8,28},{12,24},{16,4},{20,0},{24,12},{28,8},{1,21},{... | collective-permute-start | bytes 589832 | tf_op jit(solution)/shard_map/ppermute | solution.py:258
  11.5 41.5 %collective-permute-start.4 = (bf16[1024,256]{1,0:T(8,128)(2,1)S(1)}, bf16[1024,256]{1,0:T(8,128)(2,1)S(1)}, u32[]{:S(2)}, u32[]{:S(2)}) collective-permute-start(bf16[1024,256]{1,0:T(8,128)(2,1)S(1)} %bitcast.12), channel_id=1, source_target_pairs={{0,1},{1,0},{2,3},{3,2},{4,5},{5,4},{6,7},{7,6},{8,9},{9,8},{10,11... | collective-permute-start | bytes 1572872 | tf_op jit(solution)/shard_map/ppermute | solution.py:258
  21.6 31.8 %collective-permute-start.5 = (bf16[1024,256]{1,0:T(8,128)(2,1)}, bf16[1024,256]{1,0:T(8,128)(2,1)S(1)}, u32[]{:S(2)}, u32[]{:S(2)}) collective-permute-start(bf16[1024,256]{1,0:T(8,128)(2,1)} %bitcast.13), channel_id=1, source_target_pairs={{0,1},{1,0},{2,3},{3,2},{4,5},{5,4},{6,7},{7,6},{8,9},{9,8},{10,11... | collective-permute-start | bytes 1572872 | tf_op jit(solution)/shard_map/ppermute | solution.py:258
  23.2 31.8 %collective-permute-start.6 = (bf16[256,1024]{1,0:T(8,128)(2,1)}, bf16[256,1024]{1,0:T(8,128)(2,1)S(1)}, u32[]{:S(2)}, u32[]{:S(2)}) collective-permute-start(bf16[256,1024]{1,0:T(8,128)(2,1)} %bitcast.15), channel_id=1, source_target_pairs={{0,1},{1,0},{2,3},{3,2},{4,5},{5,4},{6,7},{7,6},{8,9},{9,8},{10,11... | collective-permute-start | bytes 1572872 | tf_op jit(solution)/shard_map/ppermute | solution.py:258
  23.2 16.5 %collective-permute-start.22 = (bf16[96,1024]{1,0:T(8,128)(2,1)S(1)}, bf16[96,1024]{1,0:T(8,128)(2,1)S(1)}, u32[]{:S(2)}, u32[]{:S(2)}) collective-permute-start(bf16[96,1024]{1,0:T(8,128)(2,1)S(1)} %get-tuple-element.95), channel_id=1, source_target_pairs={{0,24},{4,28},{8,16},{12,20},{16,8},{20,12},{24,0},{28,4},{1,25},{... | collective-permute-start | bytes 589832 | tf_op jit(solution)/shard_map/ppermute | solution.py:258
  29.2 14.3 %collective-permute-start.26 = (bf16[96,1024]{1,0:T(8,128)(2,1)S(1)}, bf16[96,1024]{1,0:T(8,128)(2,1)S(1)}, u32[]{:S(2)}, u32[]{:S(2)}) collective-permute-start(bf16[96,1024]{1,0:T(8,128)(2,1)S(1)} %get-tuple-element.98), channel_id=1, source_target_pairs={{0,28},{4,24},{8,20},{12,16},{16,12},{20,8},{24,4},{28,0},{1,29},{... | collective-permute-start | bytes 589832 | tf_op jit(solution)/shard_map/ppermute | solution.py:258
  39.7 7.5 %collective-permute-start.2 = (bf16[96,1024]{1,0:T(8,128)(2,1)S(1)}, bf16[96,1024]{1,0:T(8,128)(2,1)S(1)}, u32[]{:S(2)}, u32[]{:S(2)}) collective-permute-start(bf16[96,1024]{1,0:T(8,128)(2,1)S(1)} %get-tuple-element.70.refs_0_), channel_id=1, source_target_pairs={{0,2},{1,3},{2,0},{3,1},{4,6},{5,7},{6,4},{7,5},{8,10},{9,11},{10,... | collective-permute-start | bytes 589832 | tf_op jit(solution)/shard_map/ppermute | solution.py:258
  43.5 7.9 %collective-permute-start.27 = (bf16[96,1024]{1,0:T(8,128)(2,1)S(1)}, bf16[96,1024]{1,0:T(8,128)(2,1)S(1)}, u32[]{:S(2)}, u32[]{:S(2)}) collective-permute-start(bf16[96,1024]{1,0:T(8,128)(2,1)S(1)} %collective-permute-done.26.refs_0_.refs_14_), channel_id=1, source_target_pairs={{0,2},{1,3},{2,0},{3,1},{4,6},{5,7},{6,4},{7,5},{8,10},{9,11},{10,... | collective-permute-start | bytes 589832 | tf_op jit(solution)/shard_map/ppermute | solution.py:258
  47.2 11.9 %collective-permute-start.10 = (bf16[96,1024]{1,0:T(8,128)(2,1)S(1)}, bf16[96,1024]{1,0:T(8,128)(2,1)S(1)}, u32[]{:S(2)}, u32[]{:S(2)}) collective-permute-start(bf16[96,1024]{1,0:T(8,128)(2,1)S(1)} %collective-permute-done.8.refs_0_.refs_4_), channel_id=1, source_target_pairs={{0,2},{1,3},{2,0},{3,1},{4,6},{5,7},{6,4},{7,5},{8,10},{9,11},{10,... | collective-permute-start | bytes 589832 | tf_op jit(solution)/shard_map/ppermute | solution.py:258
  51.4 9.3 %collective-permute-start.11 = (bf16[96,1024]{1,0:T(8,128)(2,1)S(1)}, bf16[96,1024]{1,0:T(8,128)(2,1)S(1)}, u32[]{:S(2)}, u32[]{:S(2)}) collective-permute-start(bf16[96,1024]{1,0:T(8,128)(2,1)S(1)} %collective-permute-done.9.refs_1_.refs_5_), channel_id=1, source_target_pairs={{0,2},{1,3},{2,0},{3,1},{4,6},{5,7},{6,4},{7,5},{8,10},{9,11},{10,... | collective-permute-start | bytes 589832 | tf_op jit(solution)/shard_map/ppermute | solution.py:258
  52.9 11.1 %collective-permute-start.3 = (bf16[96,1024]{1,0:T(8,128)(2,1)S(1)}, bf16[96,1024]{1,0:T(8,128)(2,1)S(1)}, u32[]{:S(2)}, u32[]{:S(2)}) collective-permute-start(bf16[96,1024]{1,0:T(8,128)(2,1)S(1)} %collective-permute-done.1.refs_1_), channel_id=1, source_target_pairs={{0,2},{1,3},{2,0},{3,1},{4,6},{5,7},{6,4},{7,5},{8,10},{9,11},{10,... | collective-permute-start | bytes 589832 | tf_op jit(solution)/shard_map/ppermute | solution.py:258
  53.5 14.1 %collective-permute-start.23 = (bf16[96,1024]{1,0:T(8,128)(2,1)S(1)}, bf16[96,1024]{1,0:T(8,128)(2,1)S(1)}, u32[]{:S(2)}, u32[]{:S(2)}) collective-permute-start(bf16[96,1024]{1,0:T(8,128)(2,1)S(1)} %collective-permute-done.22.refs_0_.refs_12_), channel_id=1, source_target_pairs={{0,2},{1,3},{2,0},{3,1},{4,6},{5,7},{6,4},{7,5},{8,10},{9,11},{10,... | collective-permute-start | bytes 589832 | tf_op jit(solution)/shard_map/ppermute | solution.py:258
  55.0 20.5 %collective-permute-start.17 = (bf16[96,1024]{1,0:T(8,128)(2,1)S(1)}, bf16[96,1024]{1,0:T(8,128)(2,1)S(1)}, u32[]{:S(2)}, u32[]{:S(2)}) collective-permute-start(bf16[96,1024]{1,0:T(8,128)(2,1)S(1)} %collective-permute-done.15.refs_0_.refs_8_), channel_id=1, source_target_pairs={{0,2},{1,3},{2,0},{3,1},{4,6},{5,7},{6,4},{7,5},{8,10},{9,11},{10,... | collective-permute-start | bytes 589832 | tf_op jit(solution)/shard_map/ppermute | solution.py:258
  59.1 18.7 %collective-permute-start.18 = (bf16[96,1024]{1,0:T(8,128)(2,1)S(1)}, bf16[96,1024]{1,0:T(8,128)(2,1)S(1)}, u32[]{:S(2)}, u32[]{:S(2)}) collective-permute-start(bf16[96,1024]{1,0:T(8,128)(2,1)S(1)} %collective-permute-done.16.refs_1_.refs_9_), channel_id=1, source_target_pairs={{0,2},{1,3},{2,0},{3,1},{4,6},{5,7},{6,4},{7,5},{8,10},{9,11},{10,... | collective-permute-start | bytes 589832 | tf_op jit(solution)/shard_map/ppermute | solution.py:258
  60.7 13.3 %collective-permute-start.28 = (bf16[392,128]{1,0:T(8,128)(2,1)S(1)}, bf16[392,128]{1,0:T(8,128)(2,1)S(1)}, u32[]{:S(2)}, u32[]{:S(2)}) collective-permute-start(bf16[392,128]{1,0:T(8,128)(2,1)S(1)} %get-tuple-element.100), channel_id=1, source_target_pairs={{0,2},{1,3},{2,0},{3,1},{4,6},{5,7},{6,4},{7,5},{8,10},{9,11},{10,... | collective-permute-start | bytes 301064 | tf_op jit(solution)/shard_map/ppermute | solution.py:258
  64.1 20.3 %collective-permute-start.12 = (bf16[784,128]{1,0:T(8,128)(2,1)S(1)}, bf16[784,128]{1,0:T(8,128)(2,1)S(1)}, u32[]{:S(2)}, u32[]{:S(2)}) collective-permute-start(bf16[784,128]{1,0:T(8,128)(2,1)S(1)} %get-tuple-element.84), channel_id=1, source_target_pairs={{0,8},{4,12},{8,0},{12,4},{16,24},{20,28},{24,16},{28,20},{1,9},{5... | collective-permute-start | bytes 602120 | tf_op jit(solution)/shard_map/ppermute | solution.py:258
  67.6 18.3 %collective-permute-start.13 = (bf16[784,128]{1,0:T(8,128)(2,1)S(1)}, bf16[784,128]{1,0:T(8,128)(2,1)S(1)}, u32[]{:S(2)}, u32[]{:S(2)}) collective-permute-start(bf16[784,128]{1,0:T(8,128)(2,1)S(1)} %get-tuple-element.85), channel_id=1, source_target_pairs={{0,12},{4,8},{8,4},{12,0},{16,28},{20,24},{24,20},{28,16},{1,13},{... | collective-permute-start | bytes 602120 | tf_op jit(solution)/shard_map/ppermute | solution.py:258
  74.0 9.8 %collective-permute-start.24 = (bf16[392,128]{1,0:T(8,128)(2,1)S(1)}, bf16[392,128]{1,0:T(8,128)(2,1)S(1)}, u32[]{:S(2)}, u32[]{:S(2)}) collective-permute-start(bf16[392,128]{1,0:T(8,128)(2,1)S(1)} %get-tuple-element.97), channel_id=1, source_target_pairs={{0,2},{1,3},{2,0},{3,1},{4,6},{5,7},{6,4},{7,5},{8,10},{9,11},{10,... | collective-permute-start | bytes 301064 | tf_op jit(solution)/shard_map/ppermute | solution.py:258
  75.5 8.8 %collective-permute-start.29 = (bf16[392,128]{1,0:T(8,128)(2,1)S(1)}, bf16[392,128]{1,0:T(8,128)(2,1)S(1)}, u32[]{:S(2)}, u32[]{:S(2)}) collective-permute-start(bf16[392,128]{1,0:T(8,128)(2,1)S(1)} %shard_map.130), channel_id=1, source_target_pairs={{0,28},{4,24},{8,20},{12,16},{16,12},{20,8},{24,4},{28,0},{1,29},{... | collective-permute-start | bytes 301064 | tf_op jit(solution)/shard_map/ppermute | solution.py:258
  77.8 5.9 %collective-permute-start = (s32[8,128]{1,0:T(8,128)S(1)}, s32[8,128]{1,0:T(8,128)S(1)}, u32[]{:S(2)}, u32[]{:S(2)}) collective-permute-start(s32[8,128]{1,0:T(8,128)S(1)} %get-tuple-element.69), channel_id=1, source_target_pairs={{0,2},{1,3},{2,0},{3,1},{4,6},{5,7},{6,4},{7,5},{8,10},{9,11},{10,... | collective-permute-start | bytes 12296 | tf_op jit(solution)/shard_map/ppermute | solution.py:258
  83.7 30.7 %collective-permute-start.30 = (bf16[1024,256]{1,0:T(8,128)(2,1)S(1)}, bf16[1024,256]{1,0:T(8,128)(2,1)S(1)}, u32[]{:S(2)}, u32[]{:S(2)}) collective-permute-start(bf16[1024,256]{1,0:T(8,128)(2,1)S(1)} %get-tuple-element.121), channel_id=1, source_target_pairs={{0,1},{1,0},{2,3},{3,2},{4,5},{5,4},{6,7},{7,6},{8,9},{9,8},{10,11... | collective-permute-start | bytes 1572872 | tf_op jit(solution)/shard_map/ppermute | solution.py:258
  83.8 30.6 %collective-permute-start.31 = (bf16[1024,256]{1,0:T(8,128)(2,1)S(1)}, bf16[1024,256]{1,0:T(8,128)(2,1)S(1)}, u32[]{:S(2)}, u32[]{:S(2)}) collective-permute-start(bf16[1024,256]{1,0:T(8,128)(2,1)S(1)} %get-tuple-element.122), channel_id=1, source_target_pairs={{0,1},{1,0},{2,3},{3,2},{4,5},{5,4},{6,7},{7,6},{8,9},{9,8},{10,11... | collective-permute-start | bytes 1572872 | tf_op jit(solution)/shard_map/ppermute | solution.py:258
  84.3 30.1 %collective-permute-start.32 = (bf16[256,1024]{1,0:T(8,128)(2,1)S(1)}, bf16[256,1024]{1,0:T(8,128)(2,1)S(1)}, u32[]{:S(2)}, u32[]{:S(2)}) collective-permute-start(bf16[256,1024]{1,0:T(8,128)(2,1)S(1)} %get-tuple-element.123), channel_id=1, source_target_pairs={{0,1},{1,0},{2,3},{3,2},{4,5},{5,4},{6,7},{7,6},{8,9},{9,8},{10,11... | collective-permute-start | bytes 1572872 | tf_op jit(solution)/shard_map/ppermute | solution.py:258
  84.3 7.3 %collective-permute-start.7 = (bf16[784,128]{1,0:T(8,128)(2,1)S(1)}, bf16[784,128]{1,0:T(8,128)(2,1)S(1)}, u32[]{:S(2)}, u32[]{:S(2)}) collective-permute-start(bf16[784,128]{1,0:T(8,128)(2,1)S(1)} %get-tuple-element.81), channel_id=1, source_target_pairs={{0,4},{4,0},{8,12},{12,8},{16,20},{20,16},{24,28},{28,24},{1,5},{5... | collective-permute-start | bytes 602120 | tf_op jit(solution)/shard_map/ppermute | solution.py:258
  85.9 8.0 %collective-permute-start.19 = (bf16[784,128]{1,0:T(8,128)(2,1)S(1)}, bf16[784,128]{1,0:T(8,128)(2,1)S(1)}, u32[]{:S(2)}, u32[]{:S(2)}) collective-permute-start(bf16[784,128]{1,0:T(8,128)(2,1)S(1)} %get-tuple-element.92), channel_id=1, source_target_pairs={{0,2},{1,3},{2,0},{3,1},{4,6},{5,7},{6,4},{7,5},{8,10},{9,11},{10,... | collective-permute-start | bytes 602120 | tf_op jit(solution)/shard_map/ppermute | solution.py:258
  91.7 6.5 %collective-permute-start.25 = (bf16[392,128]{1,0:T(8,128)(2,1)S(1)}, bf16[392,128]{1,0:T(8,128)(2,1)S(1)}, u32[]{:S(2)}, u32[]{:S(2)}) collective-permute-start(bf16[392,128]{1,0:T(8,128)(2,1)S(1)} %shard_map.128), channel_id=1, source_target_pairs={{0,24},{4,28},{8,16},{12,20},{16,8},{20,12},{24,0},{28,4},{1,25},{... | collective-permute-start | bytes 301064 | tf_op jit(solution)/shard_map/ppermute | solution.py:258
  93.9 19.5 %collective-permute-start.14 = (bf16[136,1024]{1,0:T(8,128)(2,1)S(1)}, bf16[136,1024]{1,0:T(8,128)(2,1)S(1)}, u32[]{:S(2)}, u32[]{:S(2)}) collective-permute-start(bf16[136,1024]{1,0:T(8,128)(2,1)S(1)} %get-tuple-element.88), channel_id=1, source_target_pairs={{0,2},{1,3},{2,0},{3,1},{4,6},{5,7},{6,4},{7,5},{8,10},{9,11},{10,... | collective-permute-start | bytes 835592 | tf_op jit(solution)/shard_map/ppermute | solution.py:258
  98.2 7.8 %collective-permute-start.20 = (bf16[392,128]{1,0:T(8,128)(2,1)S(1)}, bf16[392,128]{1,0:T(8,128)(2,1)S(1)}, u32[]{:S(2)}, u32[]{:S(2)}) collective-permute-start(bf16[392,128]{1,0:T(8,128)(2,1)S(1)} %get-tuple-element.93), channel_id=1, source_target_pairs={{0,16},{4,20},{8,24},{12,28},{16,0},{20,4},{24,8},{28,12},{1,17},{... | collective-permute-start | bytes 301064 | tf_op jit(solution)/shard_map/ppermute | solution.py:258
  106.0 7.5 %collective-permute-start.21 = (bf16[392,128]{1,0:T(8,128)(2,1)S(1)}, bf16[392,128]{1,0:T(8,128)(2,1)S(1)}, u32[]{:S(2)}, u32[]{:S(2)}) collective-permute-start(bf16[392,128]{1,0:T(8,128)(2,1)S(1)} %get-tuple-element.94), channel_id=1, source_target_pairs={{0,20},{4,16},{8,28},{12,24},{16,4},{20,0},{24,12},{28,8},{1,21},{... | collective-permute-start | bytes 301064 | tf_op jit(solution)/shard_map/ppermute | solution.py:258
